TPU v7x, 512 devices: a whole 4x4x16 slice. The times are simulated.
512 devices in a mesh: grp: 16 (over y, x_hi, core), seq: 32 (over z, x_lo).
Axes of the slice: x: 4 (x_hi: 2, x_lo: 2; x = x_hi * 2 + x_lo), y: 4, z: 16, core: 2. Of those that a mesh axis runs over, the one named last changes fastest.
Arguments:
- tokens: bfloat16 [16, 4096, 1024], P('grp', 'seq'), may hold values from -40 to 40
- queries: bfloat16 [16, 4096, 512], P('grp', 'seq'), may hold values from -8 to 8
- keys: bfloat16 [16, 4096, 512], P('grp', 'seq'), may hold values from -8 to 8
- values: bfloat16 [16, 4096, 512], P('grp', 'seq'), may hold values from -6 to 6
- attn_mask: int32 [16, 32, 32], P('grp', 'seq'), may hold values from 0 to 1, as said below
- out_proj: bfloat16 [512, 1024], replicated, may hold values from -0.25 to 0.25
- norm_gain_vector: float32 [1024], replicated, may hold values from 0.5 to 1.5
- w1_packed: bfloat16 [32, 2, 128, 128], P('grp'), may hold values from -0.375 to 0.375
- w1_rows: int32 [32, 2], replicated, may hold values from 0 to 7, as said below
- w2_packed: bfloat16 [32, 2, 128, 128], P('grp'), may hold values from -0.1875 to 0.1875
- w2_cols: int32 [32, 2], replicated, may hold values from 0 to 7, as said below
- grad_out: bfloat16 [16, 4096, 1024], P('grp', 'seq'), may hold values from -6 to 6
Outputs:
- output: bfloat16 [16, 4096, 1024], P('grp', 'seq')
- grad_tokens: bfloat16 [16, 4096, 1024], P('grp', 'seq')
Inputs may be any that keep to these rules, and one draw needn't show every extreme that they name: attn_mask[s, i, i] is 1 for every sheet s and block i. `w1_rows`: the 2 entries of a row are distinct. `w2_cols`: the 2 entries of a row are distinct.
All inputs are finite; a program needn't handle non-finite values.
Results may differ from a plain program's by a relative error of at most 0.0035.
The roundings to bfloat16 on the way count: a program that leaves them out, or rounds other values in their place, can miss the bound.
Values may be sent and summed in bfloat16 or wider, within the bound.
A program may use at most 64 MiB of HBM per device.

v0:
```python
import jax
import jax.numpy as jnp
from jax import lax
from jax.sharding import PartitionSpec as P

D = 1024
HD = 64
HEADS = 8
BLK = 128


def gelu_slope(pre):
    return (
        0.5 * (1.0 + jax.scipy.special.erf(pre * 0.7071067811865476))
        + pre * jnp.exp(-0.5 * pre * pre) * 0.3989422804014327
    )


def expand_mask(mask):
    rows_blk, cols_blk = mask.shape
    wide = jnp.broadcast_to(mask[:, None, :, None], (rows_blk, BLK, cols_blk, BLK))
    return wide.reshape(rows_blk * BLK, cols_blk * BLK) > 0


def split_heads(array):
    return array.reshape(array.shape[0], HEADS, HD).transpose(1, 0, 2)


def join_heads(array):
    return array.transpose(1, 0, 2).reshape(array.shape[1], HEADS * HD)


def attend_forward(query, key_rows, value_rows, allowed):
    scale = HD ** (-0.5)

    def one_head(args):
        q_head, k_head, v_head = args
        scores = jnp.dot(q_head, k_head.T, preferred_element_type=jnp.float32) * scale
        scores = jnp.where(allowed, scores, -jnp.inf)
        top = jnp.max(scores, axis=1, keepdims=True)
        weight = jnp.exp(scores - top)
        total = jnp.sum(weight, axis=1, keepdims=True)
        prob = (weight / total).astype(jnp.bfloat16)
        return jnp.dot(prob, v_head, preferred_element_type=jnp.float32)

    heads_out = lax.map(
        one_head, (split_heads(query), split_heads(key_rows), split_heads(value_rows))
    )
    return join_heads(heads_out).astype(jnp.bfloat16)


def layer_norm_forward(hidden_state, gain_vector):
    mean_row = jnp.mean(hidden_state, axis=1, keepdims=True)
    mean_removed = hidden_state - mean_row
    reciprocal_deviation = lax.rsqrt(
        jnp.mean(mean_removed * mean_removed, axis=1, keepdims=True) + 1e-06
    )
    unit_rows = mean_removed * reciprocal_deviation
    return (unit_rows, reciprocal_deviation, (unit_rows * gain_vector).astype(jnp.bfloat16))


def layer_norm_backward(
    normed_gradient, gain_vector, unit_rows, reciprocal_deviation, gradient_rows
):
    unit_gradient = normed_gradient * gain_vector
    inner_product = (
        unit_gradient
        - jnp.mean(unit_gradient, axis=1, keepdims=True)
        - unit_rows * jnp.mean(unit_gradient * unit_rows, axis=1, keepdims=True)
    )
    return (gradient_rows.astype(jnp.float32) + reciprocal_deviation * inner_product).astype(
        jnp.bfloat16
    )


def panel_terms(first_blocks, second_blocks, row_table, col_table, normed_rows, gradient_rows):
    tok_rows = normed_rows.shape[0]
    width_blocks = D // BLK
    block_ids = jnp.arange(width_blocks, dtype=jnp.int32)[None, None, :]
    row_place = (row_table[:, :, None] == block_ids).astype(jnp.float32)
    col_place = (col_table[:, :, None] == block_ids).astype(jnp.float32)
    normed_sel = jnp.take(normed_rows.reshape(tok_rows, width_blocks, BLK), row_table, axis=1)
    pre = jnp.einsum("tcnk,cnkj->tcj", normed_sel, first_blocks, preferred_element_type=jnp.float32)
    act = jax.nn.gelu(pre, approximate=False).astype(jnp.bfloat16)
    forward_part = jnp.einsum(
        "tck,cnkj->tcnj", act, second_blocks, preferred_element_type=jnp.float32
    )
    mlp_part = jnp.einsum(
        "tcnj,cnb->tbj", forward_part, col_place, precision=lax.Precision.HIGHEST
    ).reshape(tok_rows, D)
    grad_sel = jnp.take(gradient_rows.reshape(tok_rows, width_blocks, BLK), col_table, axis=1)
    dact = jnp.einsum("tcnj,cnkj->tck", grad_sel, second_blocks, preferred_element_type=jnp.float32)
    dpre = (dact * gelu_slope(pre)).astype(jnp.bfloat16)
    back_part = jnp.einsum("tcj,cnkj->tcnk", dpre, first_blocks, preferred_element_type=jnp.float32)
    dnormed_part = jnp.einsum(
        "tcnk,cnb->tbk", back_part, row_place, precision=lax.Precision.HIGHEST
    ).reshape(tok_rows, D)
    return (mlp_part, dnormed_part)


def body(
    tokens,
    queries,
    keys,
    values,
    attn_mask,
    out_proj,
    norm_gain_vector,
    w1_packed,
    w1_rows,
    w2_packed,
    w2_cols,
    grad_out,
):
    rows_in = tokens[0]
    query = queries[0]
    gradient_rows = grad_out[0]
    allowed = expand_mask(attn_mask[0])
    key_rows, value_rows = (
        lax.all_gather(keys[0], "seq", axis=0, tiled=True),
        lax.all_gather(values[0], "seq", axis=0, tiled=True),
    )
    attn = attend_forward(query, key_rows, value_rows, allowed)
    hidden_state = rows_in.astype(jnp.float32) + jnp.dot(
        attn, out_proj, preferred_element_type=jnp.float32
    )
    unit_rows, reciprocal_deviation, normed_rows = layer_norm_forward(
        hidden_state, norm_gain_vector
    )
    first_all, second_all = (
        lax.all_gather(w1_packed, "grp", axis=0, tiled=True),
        lax.all_gather(w2_packed, "grp", axis=0, tiled=True),
    )
    mlp, normed_gradient = panel_terms(
        first_all, second_all, w1_rows, w2_cols, normed_rows, gradient_rows
    )
    result = (hidden_state + mlp).astype(jnp.bfloat16)
    incoming_gradient_rows = layer_norm_backward(
        normed_gradient, norm_gain_vector, unit_rows, reciprocal_deviation, gradient_rows
    )
    return (result[None], incoming_gradient_rows[None])


def solution(mesh):
    return jax.shard_map(
        body,
        mesh=mesh,
        in_specs=(
            P("grp", "seq", None),
            P("grp", "seq", None),
            P("grp", "seq", None),
            P("grp", "seq", None),
            P("grp", "seq", None),
            P(),
            P(),
            P("grp", None, None, None),
            P(),
            P("grp", None, None, None),
            P(),
            P("grp", "seq", None),
        ),
        out_specs=(P("grp", "seq", None), P("grp", "seq", None)),
        check_vma=False,
    )
```

profile of v0, /device:TPU:1, one launch (start us, length us, event | category | flops | bytes accessed | tf_op | source)
XLA Modules:
  0.0 497.4 jit_solution(4746874300129246282)
XLA Ops:
  7.2 1.7 copy.46
  9.0 1.7 copy.47
  10.8 0.7 all-gather.7.cloned.1.call-update
  11.5 0.5 all-gather.9.cloned.1.call-update
  12.1 0.7 compare_select_fusion.1
  12.7 0.7 compare_and_fusion.1
  13.4 0.7 compare_select_fusion
  14.1 0.7 compare_and_fusion
  14.8 1.0 copy.45
  15.8 0.7 compare_bitcast_fusion
  16.9 1.1 copy.56
  18.5 2.1 gather_fusion.1
  20.6 133.6 %all-gather.11.cloned.1.call-done = bf16[1,4096,512]{1,2,0:T(8,128)(2,1)} async-done(((bf16[1,128,512]{1,2,0:T(8,128)(2,1)}), bf16[1,4096,512]{1,2,0:T(8,128)(2,1)}) %all-gather.11.cloned.1.call-update) | async-done | bytes 4194320 | tf_op jit(solution)/shard_map/all_gather | solution.py:120
  154.2 160.8 %all-gather.13.cloned.1.call-done = bf16[1,4096,512]{1,2,0:T(8,128)(2,1)} async-done(((bf16[1,128,512]{1,2,0:T(8,128)(2,1)}), bf16[1,4096,512]{1,2,0:T(8,128)(2,1)}) %all-gather.13.cloned.1.call-update) | async-done | bytes 4194320 | tf_op jit(solution)/shard_map/all_gather | solution.py:121
  315.1 29.5 %while.11 = (s32[]{:T(128)}, bf16[8,128,64]{1,2,0:T(8,128)(2,1)S(1)}, bf16[8,128,64]{1,2,0:T(8,128)(2,1)S(1)}, bf16[8,4096,64]{1,2,0:T(8,128)(2,1)}, bf16[8,4096...) while((s32[]{:T(128)}, bf16[8,128,64]{1,2,0:T(8,128)(2,1)S(1)}, ...), condition=%wide.region_3.4_spmd.clone, body=%wide.region_0.3_spmd.clone.sunk | while | flops 138411776 | bytes 7397965 | solution.py:46
  315.1 1.6 fusion.158
  316.7 0.4 fusion.159
  317.1 1.6 fusion.160
  318.8 1.6 fusion.158
  320.4 0.4 fusion.159
  320.8 1.6 fusion.160
  322.5 1.6 fusion.158
  324.0 0.4 fusion.159
  324.5 1.6 fusion.160
  326.1 1.6 fusion.158
  327.7 0.4 fusion.159
  328.2 1.6 fusion.160
  329.8 1.6 fusion.158
  331.4 0.4 fusion.159
  331.9 1.6 fusion.160
  333.5 1.6 fusion.158
  335.1 0.4 fusion.159
  335.5 1.6 fusion.160
  337.2 1.6 fusion.158
  338.8 0.4 fusion.159
  339.2 1.6 fusion.160
  340.9 1.6 fusion.158
  342.4 0.4 fusion.159
  342.9 1.6 fusion.160
  345.4 2.2 gather_fusion
  347.6 54.0 %all-gather.7.cloned.1.call-done = bf16[32,2,128,128]{3,2,1,0:T(8,128)(2,1)} async-done(((bf16[2,2,128,128]{3,2,1,0:T(8,128)(2,1)}), bf16[32,2,128,128]{3,2,1,0:T(8,128)(2,1)}) %all-gather.7.cloned.1.call-update) | async-done | bytes 2097168 | tf_op jit(solution)/shard_map/all_gather | solution.py:131
  401.6 4.3 fusion.32
  405.9 60.7 %all-gather.9.cloned.1.call-done = bf16[32,2,128,128]{3,2,1,0:T(8,128)(2,1)} async-done(((bf16[2,2,128,128]{3,2,1,0:T(8,128)(2,1)}), bf16[32,2,128,128]{3,2,1,0:T(8,128)(2,1)}) %all-gather.9.cloned.1.call-update) | async-done | bytes 2097168 | tf_op jit(solution)/shard_map/all_gather | solution.py:132
  466.6 7.2 %convolution_bitcast_fusion.1 = f32[128,32,2,128]{3,0,2,1:T(8,128)} fusion(bf16[32,2,128,128]{3,2,1,0:T(8,128)(2,1)} %all-gather.7.cloned.1.call-done, f32[32,128,128,1]{2,1,3,0:T(8,128)} %fusion.32, bf16[32,2,128,128]{3,2,1,0:T(8,128)(2,1)} %all-gather.9.cloned.1.call-done, bf16[32,2,128,128]{3,2,1,0:T(8,128)(2,1)} %bitcast.202, pred[32,2]{1,0:T(8,128)(4,1)S(1)} %copy.55), kind=kOutput, calls=%fused_computation.24 | convolution fusion | flops 543162368 | bytes 12582976 | tf_op jit(solution)/shard_map/tcj,cnkj->tcnk/dot_general | solution.py:94
  473.8 6.7 %fusion.96 = (f32[128]{0:T(128)S(1)}, f32[8,128,128,1]{2,0,3,1:T(8,128)S(1)}) fusion(f32[8,128]{1,0:T(8,128)S(1)} %bitcast.208, f32[128,32,2,128]{3,0,2,1:T(8,128)} %convolution_bitcast_fusion.1, s32[32,2]{0,1:T(2,128)S(1)} %copy-done.5), kind=kOutput, calls=%fused_computation.111 | convolution fusion | flops 100925824 | bytes 4723456 | tf_op jit(solution)/shard_map/tcnk,cnb->tbk/dot_general | solution.py:95
  480.8 5.1 %convolution_bitcast_fusion.2 = f32[128,32,2,128]{3,0,2,1:T(8,128)S(1)} fusion(bf16[32,2,128,128]{3,2,1,0:T(8,128)(2,1)S(1)} %copy-done.7, f32[32,128,128,1]{2,1,3,0:T(8,128)S(1)} %copy-done.1), kind=kOutput, calls=%fused_computation.25 | convolution fusion | flops 302514176 | bytes 8388608 | tf_op jit(solution)/shard_map/tck,cnkj->tcnj/dot_general | solution.py:85
  485.9 3.8 fusion.15
  489.8 1.1 fusion.99
  (40 shorter events, 2.1 us)
Async XLA Ops:
  7.2 337.4 %copy-start = (bf16[512,1024]{1,0:T(8,128)(2,1)S(1)}, bf16[512,1024]{1,0:T(8,128)(2,1)}, u32[]{:S(2)}) copy-start(bf16[512,1024]{1,0:T(8,128)(2,1)} %param.21) | copy-start | bytes 3145732
  7.2 147.1 %all-gather.11.cloned.1.call-start = ((), (), s32[]{:S(2)}) async-start(), calls=%async_computation.2 | async-start | bytes 4325376 | tf_op jit(solution)/shard_map/all_gather | solution.py:120
  9.0 306.1 %all-gather.13.cloned.1.call-start = ((), (), s32[]{:S(2)}) async-start(), calls=%async_computation.3 | async-start | bytes 4325376 | tf_op jit(solution)/shard_map/all_gather | solution.py:121
  10.7 390.8 %all-gather.7.cloned.1.call-start = ((), (), s32[]{:S(2)}) async-start(), calls=%async_computation | async-start | bytes 2228224 | tf_op jit(solution)/shard_map/all_gather | solution.py:131
  11.5 455.1 %all-gather.9.cloned.1.call-start = ((), (), s32[]{:S(2)}) async-start(), calls=%async_computation.1 | async-start | bytes 2228224 | tf_op jit(solution)/shard_map/all_gather | solution.py:132
  315.1 29.5 %copy-start.3 = (bf16[1,128,1024]{2,1,0:T(8,128)(2,1)S(1)}, bf16[1,128,1024]{2,1,0:T(8,128)(2,1)}, u32[]{:S(2)}) copy-start(bf16[1,128,1024]{2,1,0:T(8,128)(2,1)} %param.16) | copy-start | bytes 786436
  344.5 0.7 copy-start.4
  466.6 7.2 %copy-start.5 = (s32[32,2]{0,1:T(2,128)S(1)}, s32[32,2]{0,1:T(2,128)}, u32[]{:S(2)}) copy-start(s32[32,2]{0,1:T(2,128)} %param.24) | copy-start | bytes 772
  473.8 7.0 %copy-start.1 = (f32[32,128,128,1]{2,1,3,0:T(8,128)S(1)}, f32[32,128,128,1]{2,1,3,0:T(8,128)}, u32[]{:S(2)}) copy-start(f32[32,128,128,1]{2,1,3,0:T(8,128)} %fusion.32) | copy-start | bytes 6291460
  473.8 7.0 %copy-start.7 = (bf16[32,2,128,128]{3,2,1,0:T(8,128)(2,1)S(1)}, bf16[32,2,128,128]{3,2,1,0:T(8,128)(2,1)}, u32[]{:S(2)}) copy-start(bf16[32,2,128,128]{3,2,1,0:T(8,128)(2,1)} %all-gather.9.cloned.1.call-done) | copy-start | bytes 6291460
  480.8 5.2 %copy-start.6 = (s32[32,2]{0,1:T(2,128)S(1)}, s32[32,2]{0,1:T(2,128)}, u32[]{:S(2)}) copy-start(s32[32,2]{0,1:T(2,128)} %param.26) | copy-start | bytes 772
  485.9 3.8 copy-start.2
Sparse Core Ops, SparseCore 0:
  10.6 143.6 all-gather.10
  156.8 158.1 all-gather.12
  318.4 83.1 all-gather.6
  404.8 61.7 all-gather.8
where the time goes:
time: 498 us; the launch traced here: 497 us
  waiting for transfers between devices  410 us (82%)
  matrix products  53.3 us (11%)
  between operations  13.9 us (3%)
  local copies, waits for them, and re-layouts  10.8 us (2%)
  other arithmetic  8.65 us (2%)
    all_gather x1, waiting for transfers between devices, body(): lax.all_gather(values[0], 'seq', axis=0, tiled=True)  161 us
    all_gather x1, waiting for transfers between devices, body(): lax.all_gather(keys[0], 'seq', axis=0, tiled=True)  134 us
    all_gather x1, waiting for transfers between devices, body(): lax.all_gather(w2_packed, 'grp', axis=0, tiled=True)  60.7 us
    all_gather x1, waiting for transfers between devices, body(): lax.all_gather(w1_packed, 'grp', axis=0, tiled=True)  54 us
    dot_general x8, matrix products, one_head(): return jnp.dot(prob, v_head, preferred_element_type=jnp.float32)  13 us
    dot_general x8, matrix products, one_head(): jnp.dot(q_head, k_head.T, preferred_element_type=jnp.float32) * scale  12.7 us
  transfers between devices with their start and end apart: 4, of which 4 were waited for; matrix products, arithmetic and copies ran while one was open for 9% of the time, Pallas kernels for 0%

commit v1 on v0

v1 whole, which is shorter than its diff:
```python
import functools

import jax
import jax.numpy as jnp
from jax import lax
from jax.experimental import pallas as pl
from jax.experimental.pallas import tpu as pltpu
from jax.sharding import PartitionSpec as P

D = 1024
HD = 64
HEADS = 8
BLK = 128
HALF = 256
LOCAL_HEADS = 4
NEG = -1e30
BF16 = jnp.bfloat16
F32 = jnp.float32

NT = (((1,), (1,)), ((), ()))


def gather_attend_kernel(
    nz,
    ny,
    q_hbm,
    k_hbm,
    v_hbm,
    mask_ref,
    w1_hbm,
    w2_hbm,
    attn_ref,
    w1_all,
    w2_all,
    kv,
    give,
    qb,
    qgive,
    wown,
    bias,
    qz,
    top,
    total,
    acc,
    ogive,
    oin,
    loc,
    kv_send,
    kv_recv,
    x_send,
    x_recv,
    y_send,
    y_recv,
    yy_send,
    yy_recv,
    wx_send,
    wx_recv,
    wc_send,
    wc_recv,
):
    grp = lax.axis_index("grp")
    seq = lax.axis_index("seq")
    z = seq // 2
    xl = seq % 2
    y = grp // 4
    xh = (grp // 2) % 2
    core = grp % 2
    half = nz // 2

    def seq_dev(zz, xx):
        return {"grp": grp, "seq": zz * 2 + xx}

    def grp_index(yy, hh, cc):
        return (yy * 2 + hh) * 2 + cc

    z_next = (z + 1) % nz
    z_prev = (z + nz - 1) % nz
    y_next = (y + 1) % ny
    y_prev = (y + ny - 1) % ny
    y_far = (y + 2) % ny
    dev_r = seq_dev(z_next, xl)
    dev_l = seq_dev(z_prev, xl)
    dev_p = seq_dev(z, 1 - xl)
    dev_yn = {"grp": grp_index(y_next, xh, core), "seq": seq}
    dev_yp = {"grp": grp_index(y_prev, xh, core), "seq": seq}
    dev_xo = {"grp": grp_index(y, 1 - xh, core), "seq": z * 2 + 1 - xl}
    dev_co = {"grp": grp_index(y, xh, 1 - core), "seq": seq}

    mine = pl.ds(pl.multiple_of(xl * HALF, HALF), HALF)
    other = pl.ds(pl.multiple_of((1 - xl) * HALF, HALF), HALF)

    w_hbm = (w1_hbm, w2_hbm)
    w_all = (w1_all, w2_all)

    def local(i):
        pairs = (
            (k_hbm.at[:, mine], kv.at[z, 0, 0]),
            (v_hbm.at[:, mine], kv.at[z, 0, 1]),
            (k_hbm.at[:, other], give.at[0]),
            (v_hbm.at[:, other], give.at[1]),
            (q_hbm.at[:, mine], qb.at[0]),
            (q_hbm.at[:, other], qgive),
            (w1_hbm, wown.at[0]),
            (w2_hbm, wown.at[1]),
            (wown.at[0], w1_all.at[pl.ds(2 * grp, 2)]),
            (wown.at[1], w2_all.at[pl.ds(2 * grp, 2)]),
        )
        return pltpu.make_async_copy(pairs[i][0], pairs[i][1], loc.at[i])

    def remote(src, dst, send, recv, device):
        return pltpu.make_async_remote_copy(
            src_ref=src,
            dst_ref=dst,
            send_sem=send,
            recv_sem=recv,
            device_id=device,
            device_id_type=pl.DeviceIdType.MESH,
        )

    for i in range(8):
        local(i).start()

    rows = lax.broadcasted_iota(jnp.int32, (32, 32), 0)
    cols = lax.broadcasted_iota(jnp.int32, (32, 32), 1)
    seen = jnp.broadcast_to(mask_ref[...].astype(F32), (32, 32))
    seen = jnp.sum(jnp.where(rows == cols, seen, 0.0), axis=1, keepdims=True)
    bias[0] = jnp.broadcast_to(jnp.where(seen == 1.0, 0.0, NEG), (32, BLK))

    barrier = pltpu.get_barrier_semaphore()
    for device in (dev_r, dev_l, dev_p, dev_yn, dev_yp, dev_xo, dev_co):
        pl.semaphore_signal(
            barrier, inc=1, device_id=device, device_id_type=pl.DeviceIdType.MESH
        )
    pl.semaphore_wait(barrier, 7)

    def kv_copy(direction, d, j):
        slot = (z + nz - d) % nz if direction == 0 else (z + d) % nz
        return remote(
            kv.at[slot, j],
            kv.at[slot, j],
            kv_send.at[direction, d, j],
            kv_recv.at[direction, d, j],
            dev_r if direction == 0 else dev_l,
        )

    def kv_landed(direction, d, j):
        slot = (z + nz - d) % nz if direction == 0 else (z + d) % nz
        return remote(
            kv.at[slot, j],
            kv.at[slot, j],
            kv_send.at[direction, d - 1, j],
            kv_recv.at[direction, d - 1, j],
            dev_r if direction == 0 else dev_l,
        )

    def w_slot(t, g):
        return w_all[t].at[pl.ds(2 * g, 2)]

    def y_copy(direction, t):
        return remote(
            wown.at[t],
            w_slot(t, grp),
            y_send.at[direction, t],
            y_recv.at[direction, t],
            dev_yn if direction == 0 else dev_yp,
        )

    def yy_copy(t):
        g = grp_index(y_prev if t == 0 else y_next, xh, core)
        return remote(
            w_slot(t, g),
            w_slot(t, g),
            yy_send.at[t],
            yy_recv.at[t],
            dev_yn if t == 0 else dev_yp,
        )

    y_of = (y, y_prev, y_next, y_far)

    def wx_copy(i, t):
        g = grp_index(y_of[i], xh, core)
        return remote(
            wown.at[t] if i == 0 else w_slot(t, g),
            w_slot(t, g),
            wx_send.at[i, t],
            wx_recv.at[i, t],
            dev_xo,
        )

    def wc_copy(i, t):
        g = grp_index(y_of[i % 4], xh if i < 4 else 1 - xh, core)
        return remote(
            wown.at[t] if i == 0 else w_slot(t, g),
            w_slot(t, g),
            wc_send.at[i, t],
            wc_recv.at[i, t],
            dev_co,
        )

    x_pairs = (
        (give, kv.at[z, 1]),
        (qgive, qb.at[1]),
        (bias.at[0], bias.at[1]),
        (ogive, oin),
    )

    def x_copy(i):
        return remote(x_pairs[i][0], x_pairs[i][1], x_send.at[i], x_recv.at[i], dev_p)

    local(2).wait()
    local(3).wait()
    x_copy(0).start()
    local(0).wait()
    local(1).wait()
    kv_copy(0, 0, 0).start()
    kv_copy(1, 0, 0).start()
    local(5).wait()
    x_copy(1).start()
    x_copy(2).start()
    local(6).wait()
    local(7).wait()
    for t in range(2):
        y_copy(0, t).start()
        y_copy(1, t).start()
        wx_copy(0, t).start()
        wc_copy(0, t).start()
        local(8 + t).start()
    x_copy(0).wait_recv()
    kv_copy(0, 0, 1).start()
    kv_copy(1, 0, 1).start()
    local(4).wait()
    x_copy(1).wait_recv()
    x_copy(2).wait_recv()

    lane = lax.broadcasted_iota(jnp.int32, (2 * BLK, BLK), 1)
    for h in range(LOCAL_HEADS):
        pair = pl.ds((h // 2) * BLK, BLK)
        both = jnp.concatenate([qb[0, :, pair], qb[1, :, pair]], axis=0).astype(F32)
        keep = (lane < HD) if h % 2 == 0 else (lane >= HD)
        qz[h] = jnp.where(keep, both * (HD**-0.5), 0.0).astype(BF16)
    top[...] = jnp.full(top.shape, NEG, F32)
    total[...] = jnp.zeros(total.shape, F32)
    acc[...] = jnp.zeros(acc.shape, F32)

    def attend(slot, p):
        pair = pl.ds(p * BLK, BLK)
        keys = jnp.concatenate([kv[slot, 0, 0, :, pair], kv[slot, 1, 0, :, pair]], axis=0)
        vals = jnp.concatenate([kv[slot, 0, 1, :, pair], kv[slot, 1, 1, :, pair]], axis=0)
        vals_t = jnp.transpose(vals)
        shift = []
        for j in range(2):
            block = slot * 2 + (xl if j == 0 else 1 - xl)
            shift.append(
                jnp.concatenate(
                    [bias[0, pl.ds(block, 1), :], bias[1, pl.ds(block, 1), :]], axis=1
                )
            )
        for u in range(2):
            h = 2 * p + u
            s = lax.dot_general(keys, qz[h], NT, preferred_element_type=F32)
            s0, s1 = s[:BLK], s[BLK:]
            old = top[h]
            new = jnp.maximum(
                jnp.max(s0, axis=0, keepdims=True) + shift[0],
                jnp.max(s1, axis=0, keepdims=True) + shift[1],
            )
            new = jnp.maximum(old, new)
            fade = jnp.exp(old - new)
            p0 = jnp.exp(s0 - (new - shift[0]))
            p1 = jnp.exp(s1 - (new - shift[1]))
            total[h] = (
                fade * total[h]
                + jnp.sum(p0, axis=0, keepdims=True)
                + jnp.sum(p1, axis=0, keepdims=True)
            )
            weight = jnp.concatenate([p0, p1], axis=0).astype(BF16)
            part = jnp.dot(
                vals_t[u * HD : (u + 1) * HD], weight, preferred_element_type=F32
            )
            acc[h] = acc[h] * fade + part
            top[h] = new

    def w_first():
        for t in range(2):
            y_copy(0, t).wait_recv()
            y_copy(1, t).wait_recv()
        yy_copy(0).start()
        yy_copy(1).start()
        for i in (1, 2):
            for t in range(2):
                wx_copy(i, t).start()
                wc_copy(i, t).start()

    def w_second():
        for t in range(2):
            yy_copy(t).wait_recv()
            wx_copy(3, t).start()
            wc_copy(3, t).start()
        for t in range(2):
            wx_copy(0, t).wait_recv()
            wc_copy(4, t).start()

    def w_third():
        for i in (1, 2):
            for t in range(2):
                wx_copy(i, t).wait_recv()
                wc_copy(4 + i, t).start()

    def w_fourth():
        for t in range(2):
            wx_copy(3, t).wait_recv()
            wc_copy(7, t).start()

    def step(d, carry):
        back = (z + nz - (d - 1)) % nz
        ahead = (z + d - 1) % nz
        inner = d < half

        kv_landed(0, d, 0).wait_recv()

        @pl.when(inner)
        def _():
            kv_copy(0, d, 0).start()

        attend(back, 0)

        @pl.when(inner)
        def _():
            kv_landed(1, d, 0).wait_recv()

        @pl.when(d < half - 1)
        def _():
            kv_copy(1, d, 0).start()

        attend(back, 1)

        @pl.when(inner)
        def _():
            kv_landed(0, d, 1).wait_recv()

        @pl.when(d < half - 1)
        def _():
            kv_copy(0, d, 1).start()

        @pl.when(d > 1)
        def _():
            attend(ahead, 0)

        kv_landed(1, d, 1).wait_recv()

        @pl.when(inner)
        def _():
            kv_copy(1, d, 1).start()

        @pl.when(d > 1)
        def _():
            attend(ahead, 1)

        pl.when(d == 1)(w_first)
        pl.when(d == 2)(w_second)
        pl.when(d == 4)(w_third)
        pl.when(d == 5)(w_fourth)
        return carry

    lax.fori_loop(1, half + 1, step, 0)
    far = (z + half) % nz
    attend(far, 0)
    attend(far, 1)

    heads_out = jnp.concatenate(
        [acc[h] / total[h] for h in range(LOCAL_HEADS)], axis=0
    )
    heads_out = jnp.transpose(heads_out).astype(BF16)
    ogive[...] = heads_out[BLK:]
    attn_ref[:, mine] = heads_out[:BLK]
    x_copy(3).start()

    for i in range(8):
        for t in range(2):
            wc_copy(i, t).wait_recv()
    for t in range(2):
        local(8 + t).wait()
        y_copy(0, t).wait_send()
        y_copy(1, t).wait_send()
        yy_copy(t).wait_send()
        for i in range(4):
            wx_copy(i, t).wait_send()
        for i in range(8):
            wc_copy(i, t).wait_send()

    def drain(d, carry):
        kv_copy(0, d, 0).wait_send()
        kv_copy(1, d, 1).wait_send()

        @pl.when(d < half - 1)
        def _():
            kv_copy(0, d, 1).wait_send()
            kv_copy(1, d, 0).wait_send()

        return carry

    lax.fori_loop(0, half, drain, 0)
    for i in range(3):
        x_copy(i).wait_send()
    x_copy(3).wait()
    attn_ref[:, other] = oin[...]


def gather_attend(nz, ny, query, key, value, mask, w1, w2):
    any_spec = pl.BlockSpec(memory_space=pl.ANY)
    vmem_spec = pl.BlockSpec(memory_space=pltpu.VMEM)
    half = nz // 2
    dma = pltpu.SemaphoreType.DMA
    fb = w1.shape[0] * ny * 4
    return pl.pallas_call(
        functools.partial(gather_attend_kernel, nz, ny),
        name="gather_attend",
        out_shape=(
            jax.ShapeDtypeStruct(query.shape, BF16),
            jax.ShapeDtypeStruct((fb,) + w1.shape[1:], BF16),
            jax.ShapeDtypeStruct((fb,) + w2.shape[1:], BF16),
        ),
        in_specs=[any_spec, any_spec, any_spec, vmem_spec, any_spec, any_spec],
        out_specs=(vmem_spec, any_spec, any_spec),
        scratch_shapes=[
            pltpu.VMEM((nz, 2, 2, BLK, HALF), BF16),
            pltpu.VMEM((2, BLK, HALF), BF16),
            pltpu.VMEM((2, BLK, HALF), BF16),
            pltpu.VMEM((BLK, HALF), BF16),
            pltpu.VMEM((2,) + w1.shape, BF16),
            pltpu.VMEM((2, 32, BLK), F32),
            pltpu.VMEM((LOCAL_HEADS, 2 * BLK, BLK), BF16),
            pltpu.VMEM((LOCAL_HEADS, 1, 2 * BLK), F32),
            pltpu.VMEM((LOCAL_HEADS, 1, 2 * BLK), F32),
            pltpu.VMEM((LOCAL_HEADS, HD, 2 * BLK), F32),
            pltpu.VMEM((BLK, HALF), BF16),
            pltpu.VMEM((BLK, HALF), BF16),
            dma((10,)),
            dma((2, half, 2)),
            dma((2, half, 2)),
            dma((4,)),
            dma((4,)),
            dma((2, 2)),
            dma((2, 2)),
            dma((2,)),
            dma((2,)),
            dma((4, 2)),
            dma((4, 2)),
            dma((8, 2)),
            dma((8, 2)),
        ],
        compiler_params=pltpu.CompilerParams(
            collective_id=0, has_side_effects=True, vmem_limit_bytes=24 << 20
        ),
    )(query, key, value, mask, w1, w2)


def mlp_kernel(
    rows_ref,
    cols_ref,
    tokens_hbm,
    attn_hbm,
    proj_hbm,
    gain_ref,
    w1_hbm,
    w2_hbm,
    grad_hbm,
    out_ref,
    gin_ref,
    tokens,
    attn,
    proj,
    w1,
    w2,
    grad,
    normed,
    gblk,
    xhat,
    mlp_acc,
    dn_acc,
    act,
    dpre,
    sems,
):
    copies = [
        pltpu.make_async_copy(src, dst, sems.at[i])
        for i, (src, dst) in enumerate(
            (
                (attn_hbm, attn),
                (proj_hbm, proj),
                (tokens_hbm, tokens),
                (grad_hbm, grad),
                (w1_hbm, w1),
                (w2_hbm, w2),
            )
        )
    ]
    for copy in copies:
        copy.start()
    for copy in copies[:3]:
        copy.wait()
    hidden = tokens[...].astype(F32) + jnp.dot(
        attn[...], proj[...], preferred_element_type=F32
    )
    mean = jnp.mean(hidden, axis=1, keepdims=True)
    removed = hidden - mean
    rstd = lax.rsqrt(jnp.mean(removed * removed, axis=1, keepdims=True) + 1e-06)
    unit = removed * rstd
    xhat[...] = unit
    normed_rows = (unit * gain_ref[...]).astype(BF16)
    db = D // BLK
    for b in range(db):
        cut = slice(b * BLK, (b + 1) * BLK)
        normed[b] = normed_rows[:, cut]
        mlp_acc[b] = hidden[:, cut]
        dn_acc[b] = jnp.zeros((BLK, BLK), F32)
    copies[3].wait()
    for b in range(db):
        gblk[b] = grad[:, b * BLK : (b + 1) * BLK]
    copies[4].wait()
    copies[5].wait()

    fb = w1.shape[0]
    group = 4

    def first(i, carry):
        for u in range(group):
            c = i * group + u
            r0, r1 = rows_ref[c, 0], rows_ref[c, 1]
            c0, c1 = cols_ref[c, 0], cols_ref[c, 1]
            picked = jnp.concatenate([normed[r0], normed[r1]], axis=1)
            pre = jnp.dot(
                picked, w1[c].reshape(2 * BLK, BLK), preferred_element_type=F32
            )
            gsel = jnp.concatenate([gblk[c0], gblk[c1]], axis=1)
            w2c = jnp.concatenate([w2[c, 0], w2[c, 1]], axis=1)
            dact = lax.dot_general(gsel, w2c, NT, preferred_element_type=F32)
            phi = 0.5 * (1.0 + lax.erf(pre * 0.7071067811865476))
            act[c] = (pre * phi).astype(BF16)
            slope = phi + pre * jnp.exp(-0.5 * pre * pre) * 0.3989422804014327
            dpre[c] = (dact * slope).astype(BF16)
        return carry

    lax.fori_loop(0, fb // group, first, 0)

    def second(i, carry):
        for u in range(group):
            c = i * group + u
            r0, r1 = rows_ref[c, 0], rows_ref[c, 1]
            c0, c1 = cols_ref[c, 0], cols_ref[c, 1]
            w2c = jnp.concatenate([w2[c, 0], w2[c, 1]], axis=1)
            fpart = jnp.dot(act[c], w2c, preferred_element_type=F32)
            mlp_acc[c0] += fpart[:, :BLK]
            mlp_acc[c1] += fpart[:, BLK:]
            bpart = lax.dot_general(
                dpre[c], w1[c].reshape(2 * BLK, BLK), NT, preferred_element_type=F32
            )
            dn_acc[r0] += bpart[:, :BLK]
            dn_acc[r1] += bpart[:, BLK:]
        return carry

    lax.fori_loop(0, fb // group, second, 0)

    for b in range(db):
        out_ref[:, b * BLK : (b + 1) * BLK] = mlp_acc[b].astype(BF16)
    dx = jnp.concatenate([dn_acc[b] for b in range(db)], axis=1) * gain_ref[...]
    unit = xhat[...]
    inner = (
        dx
        - jnp.mean(dx, axis=1, keepdims=True)
        - unit * jnp.mean(dx * unit, axis=1, keepdims=True)
    )
    gin_ref[...] = (grad[...].astype(F32) + rstd * inner).astype(BF16)


def mlp_layer(rows, cols, tokens, attn, proj, gain, w1, w2, grad):
    any_spec = pl.BlockSpec(memory_space=pl.ANY)
    vmem_spec = pl.BlockSpec(memory_space=pltpu.VMEM)
    smem_spec = pl.BlockSpec(memory_space=pltpu.SMEM)
    db = D // BLK
    fb = w1.shape[0]
    out = jax.ShapeDtypeStruct(tokens.shape, BF16)
    return pl.pallas_call(
        mlp_kernel,
        name="mlp_layer",
        out_shape=(out, out),
        in_specs=[
            smem_spec,
            smem_spec,
            any_spec,
            any_spec,
            any_spec,
            vmem_spec,
            any_spec,
            any_spec,
            any_spec,
        ],
        out_specs=(vmem_spec, vmem_spec),
        scratch_shapes=[
            pltpu.VMEM(tokens.shape, BF16),
            pltpu.VMEM(attn.shape, BF16),
            pltpu.VMEM(proj.shape, BF16),
            pltpu.VMEM(w1.shape, BF16),
            pltpu.VMEM(w2.shape, BF16),
            pltpu.VMEM(grad.shape, BF16),
            pltpu.VMEM((db, BLK, BLK), BF16),
            pltpu.VMEM((db, BLK, BLK), BF16),
            pltpu.VMEM(tokens.shape, F32),
            pltpu.VMEM((db, BLK, BLK), F32),
            pltpu.VMEM((db, BLK, BLK), F32),
            pltpu.VMEM((fb, BLK, BLK), BF16),
            pltpu.VMEM((fb, BLK, BLK), BF16),
            pltpu.SemaphoreType.DMA((6,)),
        ],
        compiler_params=pltpu.CompilerParams(vmem_limit_bytes=24 << 20),
    )(rows, cols, tokens, attn, proj, gain, w1, w2, grad)


def body(
    nz,
    ny,
    tokens,
    queries,
    keys,
    values,
    attn_mask,
    out_proj,
    norm_gain_vector,
    w1_packed,
    w1_rows,
    w2_packed,
    w2_cols,
    grad_out,
):
    attn, w1_all, w2_all = gather_attend(
        nz, ny, queries[0], keys[0], values[0], attn_mask[0], w1_packed, w2_packed
    )
    out, gin = mlp_layer(
        w1_rows,
        w2_cols,
        tokens[0],
        attn,
        out_proj,
        norm_gain_vector.reshape(1, D),
        w1_all,
        w2_all,
        grad_out[0],
    )
    return (out[None], gin[None])


def solution(mesh):
    nz = mesh.shape["seq"] // 2
    ny = mesh.shape["grp"] // 4
    return jax.shard_map(
        functools.partial(body, nz, ny),
        mesh=mesh,
        in_specs=(
            P("grp", "seq", None),
            P("grp", "seq", None),
            P("grp", "seq", None),
            P("grp", "seq", None),
            P("grp", "seq", None),
            P(),
            P(),
            P("grp", None, None, None),
            P(),
            P("grp", None, None, None),
            P(),
            P("grp", "seq", None),
        ),
        out_specs=(P("grp", "seq", None), P("grp", "seq", None)),
        check_vma=False,
    )
```

time: 498 us -> 86.2 us (0.17)
  the two profiles are of different devices: /device:TPU:1 before, /device:TPU:2 now
where the time goes in v1:
time: 86.2 us; the launch traced here: 85.9 us
  Pallas kernels  74.7 us (87%)
  local copies, waits for them, and re-layouts  10.5 us (12%)
    pallas_call x1, Pallas kernels, gather_attend(): pl.pallas_call(functools.partial(gather_attend_kernel, nz, ny), name='gat...  66.8 us
    unnamed x22, local copies, waits for them, and re-layouts  10.5 us
    pallas_call x1, Pallas kernels, mlp_layer(): pl.pallas_call(mlp_kernel, name='mlp_layer', out_shape=(out, out), in_spe...  7.87 us

profile of v1, /device:TPU:2, one launch (start us, length us, event | category | flops | bytes accessed | tf_op | source)
XLA Modules:
  0.0 85.9 jit_solution(6414934331557184747)
XLA Ops:
  0.6 0.8 copy.14.rows_ref
  1.4 0.8 copy.15.cols_ref
  2.1 0.0 copy-start.3
  2.2 0.9 %copy-done.3 = bf16[1,128,512]{2,1,0:T(8,128)(2,1)S(1)} copy-done((bf16[1,128,512]{2,1,0:T(8,128)(2,1)S(1)}, bf16[1,128,512]{2,1,0:T(8,128)(2,1)}, u32[]{:S(2)}) %copy-start.3) | copy-done | bytes 131096
  3.1 0.0 copy-start.4
  3.1 0.9 %copy-done.4 = bf16[1,128,512]{2,1,0:T(8,128)(2,1)S(1)} copy-done((bf16[1,128,512]{2,1,0:T(8,128)(2,1)S(1)}, bf16[1,128,512]{2,1,0:T(8,128)(2,1)}, u32[]{:S(2)}) %copy-start.4) | copy-done | bytes 131096
  4.0 0.0 copy-start.5
  4.0 0.9 %copy-done.5 = bf16[1,128,512]{2,1,0:T(8,128)(2,1)S(1)} copy-done((bf16[1,128,512]{2,1,0:T(8,128)(2,1)S(1)}, bf16[1,128,512]{2,1,0:T(8,128)(2,1)}, u32[]{:S(2)}) %copy-start.5) | copy-done | bytes 131096
  4.9 0.0 copy-start.6
  4.9 0.9 %copy-done.6 = bf16[2,2,128,128]{3,2,1,0:T(8,128)(2,1)S(1)} copy-done((bf16[2,2,128,128]{3,2,1,0:T(8,128)(2,1)S(1)}, bf16[2,2,128,128]{3,2,1,0:T(8,128)(2,1)}, u32[]{:S(2)}) %copy-start.6) | copy-done | bytes 131096
  5.8 0.0 copy-start.7
  5.8 0.9 %copy-done.7 = bf16[2,2,128,128]{3,2,1,0:T(8,128)(2,1)S(1)} copy-done((bf16[2,2,128,128]{3,2,1,0:T(8,128)(2,1)S(1)}, bf16[2,2,128,128]{3,2,1,0:T(8,128)(2,1)}, u32[]{:S(2)}) %copy-start.7) | copy-done | bytes 131096
  6.7 0.0 copy-start.9
  6.7 0.7 copy-done.9
  7.3 66.8 %gather_attend.1 = (bf16[128,512]{1,0:T(8,128)(2,1)S(1)}, bf16[32,2,128,128]{3,2,1,0:T(8,128)(2,1)S(1)}, bf16[32,2,128,128]{3,2,1,0:T(8,128)(2,1)S(1)}) custom-call(bf16[128,512]{1,0:T(8,128)(2,1)S(1)} %bitcast.11, bf16[128,512]{1,0:T(8,128)(2,1)S(1)} %bitcast.12, bf16[128,512]{1,0:T(8,128)(2,1)S(1)} %bitcast.13, s32[1,32]{1,0:T(1,128)S(1)} %bitcast.15, ...), custom_call_target="tpu_custom_call" | custom-call | tf_op jit(solution)/shard_map/gather_attend/pallas_call | solution.py:415
  74.2 0.0 copy-start
  74.2 1.2 %copy-done = bf16[512,1024]{1,0:T(8,128)(2,1)S(1)} copy-done((bf16[512,1024]{1,0:T(8,128)(2,1)S(1)}, bf16[512,1024]{1,0:T(8,128)(2,1)}, u32[]{:S(2)}) %copy-start) | copy-done | bytes 1048600
  75.4 0.0 copy-start.1
  75.4 0.9 %copy-done.1 = bf16[1,128,1024]{2,1,0:T(8,128)(2,1)S(1)} copy-done((bf16[1,128,1024]{2,1,0:T(8,128)(2,1)S(1)}, bf16[1,128,1024]{2,1,0:T(8,128)(2,1)}, u32[]{:S(2)}) %copy-start.1) | copy-done | bytes 262168
  76.4 0.0 copy-start.2
  76.4 0.9 %copy-done.2 = bf16[1,128,1024]{2,1,0:T(8,128)(2,1)S(1)} copy-done((bf16[1,128,1024]{2,1,0:T(8,128)(2,1)S(1)}, bf16[1,128,1024]{2,1,0:T(8,128)(2,1)}, u32[]{:S(2)}) %copy-start.2) | copy-done | bytes 262168
  77.3 0.0 copy-start.8
  77.3 0.7 copy-done.8
  78.0 7.9 %mlp_layer.1 = (bf16[128,1024]{1,0:T(8,128)(2,1)}, bf16[128,1024]{1,0:T(8,128)(2,1)}) custom-call(s32[32,2]{1,0:T(8,128)S(1)} %copy.14.rows_ref, s32[32,2]{1,0:T(8,128)S(1)} %copy.15.cols_ref, bf16[128,1024]{1,0:T(8,128)(2,1)S(1)} %bitcast.9, bf16[128,512]{1,0:T(8,128)(2,1)S(1)} %get-tuple-element.7.attn_hbm, bf16[512,1024]{1,0:T(8,128)(2,1)S(1)} %copy-done, ...), custom_call_target="tpu_custom_call" | custom-call | tf_op jit(solution)/shard_map/mlp_layer/pallas_call | solution.py:583
Async XLA Ops:
  2.1 0.9 %copy-start.3 = (bf16[1,128,512]{2,1,0:T(8,128)(2,1)S(1)}, bf16[1,128,512]{2,1,0:T(8,128)(2,1)}, u32[]{:S(2)}) copy-start(bf16[1,128,512]{2,1,0:T(8,128)(2,1)} %param.13) | copy-start | bytes 393220
  3.1 0.9 %copy-start.4 = (bf16[1,128,512]{2,1,0:T(8,128)(2,1)S(1)}, bf16[1,128,512]{2,1,0:T(8,128)(2,1)}, u32[]{:S(2)}) copy-start(bf16[1,128,512]{2,1,0:T(8,128)(2,1)} %param.14) | copy-start | bytes 393220
  4.0 0.9 %copy-start.5 = (bf16[1,128,512]{2,1,0:T(8,128)(2,1)S(1)}, bf16[1,128,512]{2,1,0:T(8,128)(2,1)}, u32[]{:S(2)}) copy-start(bf16[1,128,512]{2,1,0:T(8,128)(2,1)} %param.15) | copy-start | bytes 393220
  4.9 0.9 %copy-start.6 = (bf16[2,2,128,128]{3,2,1,0:T(8,128)(2,1)S(1)}, bf16[2,2,128,128]{3,2,1,0:T(8,128)(2,1)}, u32[]{:S(2)}) copy-start(bf16[2,2,128,128]{3,2,1,0:T(8,128)(2,1)} %w1_hbm.1) | copy-start | bytes 393220
  5.8 0.9 %copy-start.7 = (bf16[2,2,128,128]{3,2,1,0:T(8,128)(2,1)S(1)}, bf16[2,2,128,128]{3,2,1,0:T(8,128)(2,1)}, u32[]{:S(2)}) copy-start(bf16[2,2,128,128]{3,2,1,0:T(8,128)(2,1)} %w2_hbm.1) | copy-start | bytes 393220
  6.7 0.7 copy-start.9
  74.2 1.2 %copy-start = (bf16[512,1024]{1,0:T(8,128)(2,1)S(1)}, bf16[512,1024]{1,0:T(8,128)(2,1)}, u32[]{:S(2)}) copy-start(bf16[512,1024]{1,0:T(8,128)(2,1)} %proj_hbm.1) | copy-start | bytes 3145732
  75.4 0.9 %copy-start.1 = (bf16[1,128,1024]{2,1,0:T(8,128)(2,1)S(1)}, bf16[1,128,1024]{2,1,0:T(8,128)(2,1)}, u32[]{:S(2)}) copy-start(bf16[1,128,1024]{2,1,0:T(8,128)(2,1)} %param.12) | copy-start | bytes 786436
  76.4 0.9 %copy-start.2 = (bf16[1,128,1024]{2,1,0:T(8,128)(2,1)S(1)}, bf16[1,128,1024]{2,1,0:T(8,128)(2,1)}, u32[]{:S(2)}) copy-start(bf16[1,128,1024]{2,1,0:T(8,128)(2,1)} %param.23) | copy-start | bytes 786436
  77.3 0.7 copy-start.8

commit v2 on v1

v2 whole, which is shorter than its diff:
```python
import functools

import jax
import jax.numpy as jnp
from jax import lax
from jax.experimental import pallas as pl
from jax.experimental.pallas import tpu as pltpu
from jax.sharding import PartitionSpec as P

D = 1024
HD = 64
HEADS = 8
BLK = 128
HALF = 256
LOCAL_HEADS = 4
NEG = -1e30
BF16 = jnp.bfloat16
F32 = jnp.float32

NT = (((1,), (1,)), ((), ()))


def gather_attend_kernel(
    nz,
    ny,
    cols_hbm,
    q_hbm,
    k_hbm,
    v_hbm,
    mask_hbm,
    w1_hbm,
    w2_hbm,
    tokens_hbm,
    proj_hbm,
    gain_hbm,
    grad_hbm,
    hidden_ref,
    dact_ref,
    gblk,
    gain_ref,
    w1_all,
    w2_all,
    kv,
    give,
    qb,
    qgive,
    wown,
    cols_ref,
    mask,
    tokens,
    proj,
    bias,
    qz,
    top,
    total,
    acc,
    okeep,
    ogive,
    oin,
    loc,
    kv_send,
    kv_recv,
    x_send,
    x_recv,
    y_send,
    y_recv,
    yy_send,
    yy_recv,
    wx_send,
    wx_recv,
    wc_send,
    wc_recv,
):
    grp = lax.axis_index("grp")
    seq = lax.axis_index("seq")
    z = seq // 2
    xl = seq % 2
    y = grp // 4
    xh = (grp // 2) % 2
    core = grp % 2
    half = nz // 2
    db = D // BLK

    def seq_dev(zz, xx):
        return {"grp": grp, "seq": zz * 2 + xx}

    def grp_index(yy, hh, cc):
        return (yy * 2 + hh) * 2 + cc

    z_next = (z + 1) % nz
    z_prev = (z + nz - 1) % nz
    y_next = (y + 1) % ny
    y_prev = (y + ny - 1) % ny
    y_far = (y + 2) % ny
    dev_r = seq_dev(z_next, xl)
    dev_l = seq_dev(z_prev, xl)
    dev_p = seq_dev(z, 1 - xl)
    dev_yn = {"grp": grp_index(y_next, xh, core), "seq": seq}
    dev_yp = {"grp": grp_index(y_prev, xh, core), "seq": seq}
    dev_xo = {"grp": grp_index(y, 1 - xh, core), "seq": z * 2 + 1 - xl}
    dev_co = {"grp": grp_index(y, xh, 1 - core), "seq": seq}

    def columns(side, p):
        return pl.ds(pl.multiple_of(side * HALF + p * BLK, BLK), BLK)

    w_all = (w1_all, w2_all)

    pairs = []
    for p in range(2):
        pairs += [
            (k_hbm.at[:, columns(xl, p)], kv.at[p, z, 0, 0]),
            (v_hbm.at[:, columns(xl, p)], kv.at[p, z, 0, 1]),
            (k_hbm.at[:, columns(1 - xl, p)], give.at[p, 0]),
            (v_hbm.at[:, columns(1 - xl, p)], give.at[p, 1]),
            (q_hbm.at[:, columns(xl, p)], qb.at[0, p]),
            (q_hbm.at[:, columns(1 - xl, p)], qgive.at[p]),
        ]
    pairs += [
        (mask_hbm, mask),
        (w1_hbm, wown.at[0]),
        (w2_hbm, wown.at[1]),
        (wown.at[0], w1_all.at[pl.ds(2 * grp, 2)]),
        (wown.at[1], w2_all.at[pl.ds(2 * grp, 2)]),
        (proj_hbm, proj),
        (tokens_hbm, tokens),
        (gain_hbm, gain_ref),
        (cols_hbm, cols_ref),
    ]
    for b in range(db):
        pairs.append((grad_hbm.at[:, b * BLK : (b + 1) * BLK], gblk.at[b]))

    def local(i):
        return pltpu.make_async_copy(pairs[i][0], pairs[i][1], loc.at[i])

    def remote(src, dst, send, recv, device):
        return pltpu.make_async_remote_copy(
            src_ref=src,
            dst_ref=dst,
            send_sem=send,
            recv_sem=recv,
            device_id=device,
            device_id_type=pl.DeviceIdType.MESH,
        )

    for i in range(15):
        local(i).start()

    barrier = pltpu.get_barrier_semaphore()
    for device in (dev_r, dev_l, dev_p, dev_yn, dev_yp, dev_xo, dev_co):
        pl.semaphore_signal(
            barrier, inc=1, device_id=device, device_id_type=pl.DeviceIdType.MESH
        )

    local(12).wait()
    rows = lax.broadcasted_iota(jnp.int32, (32, 32), 0)
    cols = lax.broadcasted_iota(jnp.int32, (32, 32), 1)
    seen = jnp.broadcast_to(mask[...].astype(F32), (32, 32))
    seen = jnp.sum(jnp.where(rows == cols, seen, 0.0), axis=1, keepdims=True)
    bias[0] = jnp.broadcast_to(jnp.where(seen == 1.0, 0.0, NEG), (32, BLK))
    pl.semaphore_wait(barrier, 7)

    def kv_slot(direction, d):
        return (z + nz - d) % nz if direction == 0 else (z + d) % nz

    def kv_copy(direction, p, d, j):
        here = kv.at[p, kv_slot(direction, d), j]
        return remote(
            here,
            here,
            kv_send.at[direction, p, d, j],
            kv_recv.at[direction, p, d, j],
            dev_r if direction == 0 else dev_l,
        )

    def kv_landed(direction, p, d, j):
        here = kv.at[p, kv_slot(direction, d), j]
        return remote(
            here,
            here,
            kv_send.at[direction, p, d - 1, j],
            kv_recv.at[direction, p, d - 1, j],
            dev_r if direction == 0 else dev_l,
        )

    def w_slot(t, g):
        return w_all[t].at[pl.ds(2 * g, 2)]

    def y_copy(direction, t):
        return remote(
            wown.at[t],
            w_slot(t, grp),
            y_send.at[direction, t],
            y_recv.at[direction, t],
            dev_yn if direction == 0 else dev_yp,
        )

    def yy_copy(t):
        g = grp_index(y_prev if t == 0 else y_next, xh, core)
        return remote(
            w_slot(t, g),
            w_slot(t, g),
            yy_send.at[t],
            yy_recv.at[t],
            dev_yn if t == 0 else dev_yp,
        )

    y_of = (y, y_prev, y_next, y_far)

    def wx_copy(i, t):
        g = grp_index(y_of[i], xh, core)
        return remote(
            wown.at[t] if i == 0 else w_slot(t, g),
            w_slot(t, g),
            wx_send.at[i, t],
            wx_recv.at[i, t],
            dev_xo,
        )

    def wc_copy(i, t):
        g = grp_index(y_of[i % 4], xh if i < 4 else 1 - xh, core)
        return remote(
            wown.at[t] if i == 0 else w_slot(t, g),
            w_slot(t, g),
            wc_send.at[i, t],
            wc_recv.at[i, t],
            dev_co,
        )

    x_pairs = (
        (give.at[0], kv.at[0, z, 1]),
        (give.at[1], kv.at[1, z, 1]),
        (qgive, qb.at[1]),
        (bias.at[0], bias.at[1]),
        (ogive.at[0], oin.at[0]),
        (ogive.at[1], oin.at[1]),
    )

    def x_copy(i):
        return remote(x_pairs[i][0], x_pairs[i][1], x_send.at[i], x_recv.at[i], dev_p)

    for p in range(2):
        local(6 * p).wait()
        local(6 * p + 1).wait()
        kv_copy(0, p, 0, 0).start()
        kv_copy(1, p, 0, 0).start()
        local(6 * p + 2).wait()
        local(6 * p + 3).wait()
        x_copy(p).start()
    local(5).wait()
    local(11).wait()
    x_copy(2).start()
    x_copy(3).start()
    local(13).wait()
    local(14).wait()
    for t in range(2):
        y_copy(0, t).start()
        y_copy(1, t).start()
        wx_copy(0, t).start()
        wc_copy(0, t).start()
        local(15 + t).start()
    for i in range(17, len(pairs)):
        local(i).start()
    for p in range(2):
        x_copy(p).wait_recv()
        kv_copy(0, p, 0, 1).start()
        kv_copy(1, p, 0, 1).start()
    local(4).wait()
    local(10).wait()
    x_copy(2).wait_recv()
    x_copy(3).wait_recv()

    lane = lax.broadcasted_iota(jnp.int32, (2 * BLK, BLK), 1)
    for h in range(LOCAL_HEADS):
        both = jnp.concatenate([qb[0, h // 2], qb[1, h // 2]], axis=0).astype(F32)
        keep = (lane < HD) if h % 2 == 0 else (lane >= HD)
        qz[h] = jnp.where(keep, both * (HD**-0.5), 0.0).astype(BF16)
    top[...] = jnp.full(top.shape, NEG, F32)
    total[...] = jnp.zeros(total.shape, F32)
    acc[...] = jnp.zeros(acc.shape, F32)

    def attend(slot, p):
        keys = jnp.concatenate([kv[p, slot, 0, 0], kv[p, slot, 1, 0]], axis=0)
        vals = jnp.concatenate([kv[p, slot, 0, 1], kv[p, slot, 1, 1]], axis=0)
        vals_t = jnp.transpose(vals)
        shift = []
        for j in range(2):
            block = slot * 2 + (xl if j == 0 else 1 - xl)
            shift.append(
                jnp.concatenate(
                    [bias[0, pl.ds(block, 1), :], bias[1, pl.ds(block, 1), :]], axis=1
                )
            )
        for u in range(2):
            h = 2 * p + u
            s = lax.dot_general(keys, qz[h], NT, preferred_element_type=F32)
            s0, s1 = s[:BLK], s[BLK:]
            old = top[h]
            new = jnp.maximum(
                jnp.max(s0, axis=0, keepdims=True) + shift[0],
                jnp.max(s1, axis=0, keepdims=True) + shift[1],
            )
            new = jnp.maximum(old, new)
            fade = jnp.exp(old - new)
            p0 = jnp.exp(s0 - (new - shift[0]))
            p1 = jnp.exp(s1 - (new - shift[1]))
            total[h] = (
                fade * total[h]
                + jnp.sum(p0, axis=0, keepdims=True)
                + jnp.sum(p1, axis=0, keepdims=True)
            )
            weight = jnp.concatenate([p0, p1], axis=0).astype(BF16)
            part = jnp.dot(
                vals_t[u * HD : (u + 1) * HD], weight, preferred_element_type=F32
            )
            acc[h] = acc[h] * fade + part
            top[h] = new

    def finish(p):
        out = jnp.concatenate(
            [acc[2 * p + u] * (1.0 / total[2 * p + u]) for u in range(2)], axis=0
        )
        out = jnp.transpose(out).astype(BF16)
        ogive[p] = out[BLK:]
        okeep[p] = out[:BLK]
        x_copy(4 + p).start()

    def project(value, side):
        return jnp.dot(
            jnp.concatenate([value[0], value[1]], axis=1),
            proj[pl.ds(pl.multiple_of(side * HALF, HALF), HALF), :],
            preferred_element_type=F32,
        )

    def w_first():
        for t in range(2):
            y_copy(0, t).wait_recv()
            y_copy(1, t).wait_recv()
        yy_copy(0).start()
        yy_copy(1).start()
        for i in (1, 2):
            for t in range(2):
                wx_copy(i, t).start()
                wc_copy(i, t).start()

    def w_second():
        for t in range(2):
            yy_copy(t).wait_recv()
            wx_copy(3, t).start()
            wc_copy(3, t).start()
        for t in range(2):
            wx_copy(0, t).wait_recv()
            wc_copy(4, t).start()

    def w_third():
        for i in (1, 2):
            for t in range(2):
                wx_copy(i, t).wait_recv()
                wc_copy(4 + i, t).start()

    def w_fourth():
        for t in range(2):
            wx_copy(3, t).wait_recv()
            wc_copy(7, t).start()

    def w_done():
        for i in range(8):
            for t in range(2):
                wc_copy(i, t).wait_recv()
        for i in range(15, 17):
            local(i).wait()
        for i in range(19, len(pairs)):
            local(i).wait()

    fb = w1_all.shape[0]
    portion = fb // 2

    def back_dact(first):
        def one(u, carry):
            c = first + u
            c0, c1 = cols_ref[0, c], cols_ref[1, c]
            gsel = jnp.concatenate([gblk[c0], gblk[c1]], axis=1)
            w2c = jnp.concatenate([w2_all[c, 0], w2_all[c, 1]], axis=1)
            dact_ref[c] = lax.dot_general(gsel, w2c, NT, preferred_element_type=F32)
            return carry

        lax.fori_loop(0, portion, one, 0)

    def step(d, carry):
        back = (z + nz - (d - 1)) % nz
        ahead = (z + d - 1) % nz
        more = d < half - 1

        for k, (j, p) in enumerate(((0, 0), (0, 1), (1, 0), (1, 1))):
            far_dir = j
            near_dir = 1 - j
            kv_landed(far_dir, p, d, j).wait_recv()
            kv_copy(far_dir, p, d, j).start()
            kv_landed(near_dir, p, d, j).wait_recv()

            @pl.when(more)
            def _(near_dir=near_dir, p=p, j=j):
                kv_copy(near_dir, p, d, j).start()

            if k < 2:
                attend(back, k)
            else:

                @pl.when(d > 1)
                def _(k=k):
                    attend(ahead, k - 2)

        pl.when(d == 1)(w_first)
        pl.when(d == 2)(w_second)
        pl.when(d == 4)(w_third)
        pl.when(d == 5)(w_fourth)
        pl.when(d == half - 2)(w_done)

        @pl.when(d > half - 3)
        def _():
            back_dact((d - half + 2) * portion)

        return carry

    lax.fori_loop(1, half, step, 0)

    def rest(i, carry):
        slot = jnp.where(i < 2, z + nz - (half - 1), z + half - 1) % nz
        attend(slot, i % 2)
        return carry

    lax.fori_loop(0, 4, rest, 0)
    local(17).wait()
    local(18).wait()
    for p in range(2):
        kv_landed(0, p, half, 0).wait_recv()
        kv_landed(1, p, half, 1).wait_recv()
        attend((z + half) % nz, p)
        finish(p)
    hidden_ref[...] = tokens[...].astype(F32) + project(okeep, xl)

    for t in range(2):
        y_copy(0, t).wait_send()
        y_copy(1, t).wait_send()
        yy_copy(t).wait_send()
        for i in range(4):
            wx_copy(i, t).wait_send()
        for i in range(8):
            wc_copy(i, t).wait_send()

    def drain(d, carry):
        for p in range(2):
            kv_copy(0, p, d, 0).wait_send()
            kv_copy(1, p, d, 1).wait_send()

        @pl.when(d < half - 1)
        def _():
            for p in range(2):
                kv_copy(0, p, d, 1).wait_send()
                kv_copy(1, p, d, 0).wait_send()

        return carry

    lax.fori_loop(0, half, drain, 0)
    for i in range(4):
        x_copy(i).wait_send()
    x_copy(4).wait()
    x_copy(5).wait()
    hidden_ref[...] += project(oin, 1 - xl)


def gather_attend(nz, ny, cols, query, key, value, mask, w1, w2, tokens, proj, gain, grad):
    hbm_spec = pl.BlockSpec(memory_space=pltpu.HBM)
    vmem_spec = pl.BlockSpec(memory_space=pltpu.VMEM)
    half = nz // 2
    db = D // BLK
    dma = pltpu.SemaphoreType.DMA
    fb = w1.shape[0] * ny * 4
    return pl.pallas_call(
        functools.partial(gather_attend_kernel, nz, ny),
        name="gather_attend",
        out_shape=(
            jax.ShapeDtypeStruct(tokens.shape, F32),
            jax.ShapeDtypeStruct((fb, BLK, BLK), F32),
            jax.ShapeDtypeStruct((db, BLK, BLK), BF16),
            jax.ShapeDtypeStruct(gain.shape, F32),
            jax.ShapeDtypeStruct((fb,) + w1.shape[1:], BF16),
            jax.ShapeDtypeStruct((fb,) + w2.shape[1:], BF16),
        ),
        in_specs=[hbm_spec] * 11,
        out_specs=(vmem_spec,) * 6,
        scratch_shapes=[
            pltpu.VMEM((2, nz, 2, 2, BLK, BLK), BF16),
            pltpu.VMEM((2, 2, BLK, BLK), BF16),
            pltpu.VMEM((2, 2, BLK, BLK), BF16),
            pltpu.VMEM((2, BLK, BLK), BF16),
            pltpu.VMEM((2,) + w1.shape, BF16),
            pltpu.SMEM(cols.shape, cols.dtype),
            pltpu.VMEM(mask.shape, mask.dtype),
            pltpu.VMEM(tokens.shape, BF16),
            pltpu.VMEM(proj.shape, BF16),
            pltpu.VMEM((2, 32, BLK), F32),
            pltpu.VMEM((LOCAL_HEADS, 2 * BLK, BLK), BF16),
            pltpu.VMEM((LOCAL_HEADS, 1, 2 * BLK), F32),
            pltpu.VMEM((LOCAL_HEADS, 1, 2 * BLK), F32),
            pltpu.VMEM((LOCAL_HEADS, HD, 2 * BLK), F32),
            pltpu.VMEM((2, BLK, BLK), BF16),
            pltpu.VMEM((2, BLK, BLK), BF16),
            pltpu.VMEM((2, BLK, BLK), BF16),
            dma((21 + db,)),
            dma((2, 2, half, 2)),
            dma((2, 2, half, 2)),
            dma((6,)),
            dma((6,)),
            dma((2, 2)),
            dma((2, 2)),
            dma((2,)),
            dma((2,)),
            dma((4, 2)),
            dma((4, 2)),
            dma((8, 2)),
            dma((8, 2)),
        ],
        compiler_params=pltpu.CompilerParams(
            collective_id=0, has_side_effects=True, vmem_limit_bytes=32 << 20
        ),
    )(
        *(
            pltpu.with_memory_space_constraint(x, pltpu.HBM)
            for x in (cols, query, key, value, mask, w1, w2, tokens, proj, gain, grad)
        ),
    )


def mlp_kernel(
    rows_ref,
    cols_ref,
    hidden_ref,
    dact_ref,
    gblk,
    gain_ref,
    w1,
    w2,
    out_ref,
    gin_ref,
    normed,
    xhat,
    mlp_acc,
    dn_acc,
    act,
    dpre,
):
    hidden = hidden_ref[...]
    mean = jnp.mean(hidden, axis=1, keepdims=True)
    removed = hidden - mean
    rstd = lax.rsqrt(jnp.mean(removed * removed, axis=1, keepdims=True) + 1e-06)
    unit = removed * rstd
    xhat[...] = unit
    normed_rows = (unit * gain_ref[...]).astype(BF16)
    db = D // BLK
    for b in range(db):
        cut = slice(b * BLK, (b + 1) * BLK)
        normed[b] = normed_rows[:, cut]
        mlp_acc[b] = hidden[:, cut]
        dn_acc[b] = jnp.zeros((BLK, BLK), F32)

    fb = w1.shape[0]
    group = 4

    def first(i, carry):
        for u in range(group):
            c = i * group + u
            picked = jnp.concatenate(
                [normed[rows_ref[0, c]], normed[rows_ref[1, c]]], axis=1
            )
            pre = jnp.dot(
                picked, w1[c].reshape(2 * BLK, BLK), preferred_element_type=F32
            )
            phi = 0.5 * (1.0 + lax.erf(pre * 0.7071067811865476))
            act[c] = (pre * phi).astype(BF16)
            slope = phi + pre * jnp.exp(-0.5 * pre * pre) * 0.3989422804014327
            dpre[c] = (dact_ref[c] * slope).astype(BF16)
        return carry

    lax.fori_loop(0, fb // group, first, 0)

    def second(i, carry):
        for u in range(group):
            c = i * group + u
            w2c = jnp.concatenate([w2[c, 0], w2[c, 1]], axis=1)
            fpart = jnp.dot(act[c], w2c, preferred_element_type=F32)
            mlp_acc[cols_ref[0, c]] += fpart[:, :BLK]
            mlp_acc[cols_ref[1, c]] += fpart[:, BLK:]
            bpart = lax.dot_general(
                dpre[c], w1[c].reshape(2 * BLK, BLK), NT, preferred_element_type=F32
            )
            dn_acc[rows_ref[0, c]] += bpart[:, :BLK]
            dn_acc[rows_ref[1, c]] += bpart[:, BLK:]
        return carry

    lax.fori_loop(0, fb // group, second, 0)

    for b in range(db):
        out_ref[:, b * BLK : (b + 1) * BLK] = mlp_acc[b].astype(BF16)
    dx = jnp.concatenate([dn_acc[b] for b in range(db)], axis=1) * gain_ref[...]
    unit = xhat[...]
    inner = (
        dx
        - jnp.mean(dx, axis=1, keepdims=True)
        - unit * jnp.mean(dx * unit, axis=1, keepdims=True)
    )
    grad = jnp.concatenate([gblk[b] for b in range(db)], axis=1)
    gin_ref[...] = (grad.astype(F32) + rstd * inner).astype(BF16)


def mlp_layer(rows, cols, hidden, dact, gblk, gain, w1, w2):
    vmem_spec = pl.BlockSpec(memory_space=pltpu.VMEM)
    smem_spec = pl.BlockSpec(memory_space=pltpu.SMEM)
    db = D // BLK
    fb = w1.shape[0]
    out = jax.ShapeDtypeStruct(hidden.shape, BF16)
    return pl.pallas_call(
        mlp_kernel,
        name="mlp_layer",
        out_shape=(out, out),
        in_specs=[smem_spec, smem_spec] + [vmem_spec] * 6,
        out_specs=(vmem_spec, vmem_spec),
        scratch_shapes=[
            pltpu.VMEM((db, BLK, BLK), BF16),
            pltpu.VMEM(hidden.shape, F32),
            pltpu.VMEM((db, BLK, BLK), F32),
            pltpu.VMEM((db, BLK, BLK), F32),
            pltpu.VMEM((fb, BLK, BLK), BF16),
            pltpu.VMEM((fb, BLK, BLK), BF16),
        ],
        compiler_params=pltpu.CompilerParams(vmem_limit_bytes=32 << 20),
    )(rows, cols, hidden, dact, gblk, gain, w1, w2)


def body(
    nz,
    ny,
    tokens,
    queries,
    keys,
    values,
    attn_mask,
    out_proj,
    norm_gain_vector,
    w1_packed,
    w1_rows,
    w2_packed,
    w2_cols,
    grad_out,
):
    rows, cols = w1_rows.T, w2_cols.T
    hidden, dact, gblk, gain, w1_all, w2_all = gather_attend(
        nz,
        ny,
        cols,
        queries[0],
        keys[0],
        values[0],
        attn_mask[0],
        w1_packed,
        w2_packed,
        tokens[0],
        out_proj,
        norm_gain_vector.reshape(1, D),
        grad_out[0],
    )
    out, gin = mlp_layer(rows, cols, hidden, dact, gblk, gain, w1_all, w2_all)
    return (out[None], gin[None])


def solution(mesh):
    nz = mesh.shape["seq"] // 2
    ny = mesh.shape["grp"] // 4
    return jax.shard_map(
        functools.partial(body, nz, ny),
        mesh=mesh,
        in_specs=(
            P("grp", "seq", None),
            P("grp", "seq", None),
            P("grp", "seq", None),
            P("grp", "seq", None),
            P("grp", "seq", None),
            P(),
            P(),
            P("grp", None, None, None),
            P(),
            P("grp", None, None, None),
            P(),
            P("grp", "seq", None),
        ),
        out_specs=(P("grp", "seq", None), P("grp", "seq", None)),
        check_vma=False,
    )
```

time: 86.2 us -> 75.8 us (0.88)
  local copies, waits for them, and re-layouts: 10.5 us -> 0.01 us
    unnamed x22 -> x4, local copies, waits for them, and re-layouts: 10.5 us -> 0.01 us
    pallas_call x1, Pallas kernels: 66.8 us -> 68.4 us  [gather_attend(): pl.pallas_call(functools.partial(gather_attend_kernel, nz, ny), name='gat...]
    pallas_call x1, Pallas kernels: 7.87 us -> 6.56 us  [mlp_layer(): pl.pallas_call(mlp_kernel, name='mlp_layer', out_shape=(out, out), in_spe...]
where the time goes in v2:
time: 75.8 us; the launch traced here: 75.6 us
  Pallas kernels  75 us (99%)
    pallas_call x1, Pallas kernels, gather_attend(): pl.pallas_call(functools.partial(gather_attend_kernel, nz, ny), name='gat...  68.4 us
    pallas_call x1, Pallas kernels, mlp_layer(): pl.pallas_call(mlp_kernel, name='mlp_layer', out_shape=(out, out), in_spe...  6.56 us

profile of v2, /device:TPU:2, one launch (start us, length us, event | category | flops | bytes accessed | tf_op | source)
XLA Modules:
  0.0 75.6 jit_solution(14271819369257405770)
XLA Ops:
  0.6 0.0 copy-start
  0.6 0.0 copy-start.1
  0.7 68.4 %gather_attend.1 = (f32[128,1024]{1,0:T(8,128)S(1)}, f32[32,128,128]{2,1,0:T(8,128)S(1)}, bf16[8,128,128]{2,1,0:T(8,128)(2,1)S(1)}, f32[1,1024]{1,0:T(1,128)S(1)...) custom-call(s32[2,32]{1,0:T(2,128)} %bitcast.11, bf16[128,512]{1,0:T(8,128)(2,1)} %bitcast.16, ...), custom_call_target="tpu_custom_call" | custom-call | tf_op jit(solution)/shard_map/gather_attend/pallas_call | solution.py:478
  69.1 0.0 copy-done
  69.1 0.0 copy-done.1
  69.1 6.6 %mlp_layer.1 = (bf16[128,1024]{1,0:T(8,128)(2,1)}, bf16[128,1024]{1,0:T(8,128)(2,1)}) custom-call(s32[2,32]{1,0:T(2,128)S(1)} %bitcast.13, s32[2,32]{1,0:T(2,128)S(1)} %bitcast.12, f32[128,1024]{1,0:T(8,128)S(1)} %get-tuple-element.10.hidden_ref, f32[32,128,128]{2,1,0:T(8,128)S(1)} %get-tuple-element.11.dact_ref, ...), custom_call_target="tpu_custom_call" | custom-call | tf_op jit(solution)/shard_map/mlp_layer/pallas_call | solution.py:621
Async XLA Ops:
  0.6 68.4 %copy-start = (s32[32,2]{0,1:T(2,128)S(1)}, s32[32,2]{0,1:T(2,128)}, u32[]{:S(2)}) copy-start(s32[32,2]{0,1:T(2,128)} %param.22) | copy-start | bytes 772
  0.6 68.4 %copy-start.1 = (s32[32,2]{0,1:T(2,128)S(1)}, s32[32,2]{0,1:T(2,128)}, u32[]{:S(2)}) copy-start(s32[32,2]{0,1:T(2,128)} %param.20) | copy-start | bytes 772

commit v3 on v2

--- a/solution.py
+++ b/solution.py
@@ -41,9 +41,7 @@
     w1_all,
     w2_all,
     kv,
-    give,
     qb,
-    qgive,
     wown,
     cols_ref,
     mask,
@@ -110,10 +108,7 @@
         pairs += [
             (k_hbm.at[:, columns(xl, p)], kv.at[p, z, 0, 0]),
             (v_hbm.at[:, columns(xl, p)], kv.at[p, z, 0, 1]),
-            (k_hbm.at[:, columns(1 - xl, p)], give.at[p, 0]),
-            (v_hbm.at[:, columns(1 - xl, p)], give.at[p, 1]),
             (q_hbm.at[:, columns(xl, p)], qb.at[0, p]),
-            (q_hbm.at[:, columns(1 - xl, p)], qgive.at[p]),
         ]
     pairs += [
         (mask_hbm, mask),
@@ -121,8 +116,8 @@
         (w2_hbm, wown.at[1]),
         (wown.at[0], w1_all.at[pl.ds(2 * grp, 2)]),
         (wown.at[1], w2_all.at[pl.ds(2 * grp, 2)]),
+        (tokens_hbm, tokens),
         (proj_hbm, proj),
-        (tokens_hbm, tokens),
         (gain_hbm, gain_ref),
         (cols_hbm, cols_ref),
     ]
@@ -142,16 +137,15 @@
             device_id_type=pl.DeviceIdType.MESH,
         )
 
-    for i in range(15):
-        local(i).start()
-
     barrier = pltpu.get_barrier_semaphore()
     for device in (dev_r, dev_l, dev_p, dev_yn, dev_yp, dev_xo, dev_co):
         pl.semaphore_signal(
             barrier, inc=1, device_id=device, device_id_type=pl.DeviceIdType.MESH
         )
-
-    local(12).wait()
+    for i in (6, 7, 8, 0, 1, 2, 3, 4, 5):
+        local(i).start()
+
+    local(6).wait()
     rows = lax.broadcasted_iota(jnp.int32, (32, 32), 0)
     cols = lax.broadcasted_iota(jnp.int32, (32, 32), 1)
     seen = jnp.broadcast_to(mask[...].astype(F32), (32, 32))
@@ -227,9 +221,9 @@
         )
 
     x_pairs = (
-        (give.at[0], kv.at[0, z, 1]),
-        (give.at[1], kv.at[1, z, 1]),
-        (qgive, qb.at[1]),
+        (kv.at[0, z, 0], kv.at[0, z, 1]),
+        (kv.at[1, z, 0], kv.at[1, z, 1]),
+        (qb.at[0], qb.at[1]),
         (bias.at[0], bias.at[1]),
         (ogive.at[0], oin.at[0]),
         (ogive.at[1], oin.at[1]),
@@ -238,34 +232,50 @@
     def x_copy(i):
         return remote(x_pairs[i][0], x_pairs[i][1], x_send.at[i], x_recv.at[i], dev_p)
 
+    kv_hbm = (k_hbm, v_hbm)
     for p in range(2):
-        local(6 * p).wait()
-        local(6 * p + 1).wait()
-        kv_copy(0, p, 0, 0).start()
-        kv_copy(1, p, 0, 0).start()
-        local(6 * p + 2).wait()
-        local(6 * p + 3).wait()
-        x_copy(p).start()
-    local(5).wait()
-    local(11).wait()
-    x_copy(2).start()
+        for direction in range(2):
+            for i in range(2):
+                remote(
+                    kv_hbm[i].at[:, columns(xl, p)],
+                    kv.at[p, z, 0, i],
+                    kv_send.at[direction, p, 0, 0],
+                    kv_recv.at[direction, p, 0, 0],
+                    dev_r if direction == 0 else dev_l,
+                ).start()
+        for i in range(2):
+            remote(
+                kv_hbm[i].at[:, columns(1 - xl, p)],
+                kv.at[p, z, 1, i],
+                x_send.at[p],
+                x_recv.at[p],
+                dev_p,
+            ).start()
+    for p in range(2):
+        remote(
+            q_hbm.at[:, columns(1 - xl, p)],
+            qb.at[1, p],
+            x_send.at[2],
+            x_recv.at[2],
+            dev_p,
+        ).start()
     x_copy(3).start()
-    local(13).wait()
-    local(14).wait()
+    local(7).wait()
+    local(8).wait()
     for t in range(2):
         y_copy(0, t).start()
         y_copy(1, t).start()
         wx_copy(0, t).start()
         wc_copy(0, t).start()
-        local(15 + t).start()
-    for i in range(17, len(pairs)):
-        local(i).start()
+        local(9 + t).start()
     for p in range(2):
         x_copy(p).wait_recv()
         kv_copy(0, p, 0, 1).start()
         kv_copy(1, p, 0, 1).start()
-    local(4).wait()
-    local(10).wait()
+    for i in range(11, len(pairs)):
+        local(i).start()
+    for i in range(6):
+        local(i).wait()
     x_copy(2).wait_recv()
     x_copy(3).wait_recv()
 
@@ -290,30 +300,38 @@
                     [bias[0, pl.ds(block, 1), :], bias[1, pl.ds(block, 1), :]], axis=1
                 )
             )
-        for u in range(2):
-            h = 2 * p + u
-            s = lax.dot_general(keys, qz[h], NT, preferred_element_type=F32)
-            s0, s1 = s[:BLK], s[BLK:]
-            old = top[h]
-            new = jnp.maximum(
-                jnp.max(s0, axis=0, keepdims=True) + shift[0],
-                jnp.max(s1, axis=0, keepdims=True) + shift[1],
-            )
-            new = jnp.maximum(old, new)
+        cuts = (slice(0, BLK), slice(BLK, 2 * BLK))
+        chains = [(u, cut) for u in range(2) for cut in cuts]
+        state = [
+            (top[2 * p + u][:, cut], total[2 * p + u][:, cut], acc[2 * p + u, :, cut])
+            for u, cut in chains
+        ]
+        scores = [
+            lax.dot_general(keys, qz[2 * p + u, cut], NT, preferred_element_type=F32)
+            for u, cut in chains
+        ]
+        ready = []
+        for (u, cut), (old, tot, part), s in zip(chains, state, scores):
+            move = [x[:, cut] for x in shift]
+            new = old
+            for j in range(2):
+                peak = jnp.max(s[j * BLK : (j + 1) * BLK], axis=0, keepdims=True)
+                new = jnp.maximum(new, peak + move[j])
             fade = jnp.exp(old - new)
-            p0 = jnp.exp(s0 - (new - shift[0]))
-            p1 = jnp.exp(s1 - (new - shift[1]))
-            total[h] = (
-                fade * total[h]
-                + jnp.sum(p0, axis=0, keepdims=True)
-                + jnp.sum(p1, axis=0, keepdims=True)
-            )
-            weight = jnp.concatenate([p0, p1], axis=0).astype(BF16)
-            part = jnp.dot(
+            tot = fade * tot
+            weight = []
+            for j in range(2):
+                w = jnp.exp(s[j * BLK : (j + 1) * BLK] - (new - move[j]))
+                tot = tot + jnp.sum(w, axis=0, keepdims=True)
+                weight.append(w)
+            weight = jnp.concatenate(weight, axis=0).astype(BF16)
+            ready.append((new, tot, part * fade, weight))
+        for (u, cut), (new, tot, part, weight) in zip(chains, ready):
+            acc[2 * p + u, :, cut] = part + jnp.dot(
                 vals_t[u * HD : (u + 1) * HD], weight, preferred_element_type=F32
             )
-            acc[h] = acc[h] * fade + part
-            top[h] = new
+            top[2 * p + u, :, cut] = new
+            total[2 * p + u, :, cut] = tot
 
     def finish(p):
         out = jnp.concatenate(
@@ -366,13 +384,13 @@
         for i in range(8):
             for t in range(2):
                 wc_copy(i, t).wait_recv()
-        for i in range(15, 17):
+        for i in range(9, 11):
             local(i).wait()
-        for i in range(19, len(pairs)):
+        for i in range(13, len(pairs)):
             local(i).wait()
 
     fb = w1_all.shape[0]
-    portion = fb // 2
+    portion = fb // 4
 
     def back_dact(first):
         def one(u, carry):
@@ -386,7 +404,7 @@
         lax.fori_loop(0, portion, one, 0)
 
     def step(d, carry):
-        back = (z + nz - (d - 1)) % nz
+        back = (z + nz - d) % nz
         ahead = (z + d - 1) % nz
         more = d < half - 1
 
@@ -401,36 +419,25 @@
             def _(near_dir=near_dir, p=p, j=j):
                 kv_copy(near_dir, p, d, j).start()
 
-            if k < 2:
-                attend(back, k)
-            else:
-
-                @pl.when(d > 1)
-                def _(k=k):
-                    attend(ahead, k - 2)
+            if k == 0:
+                pl.when(d == 5)(w_fourth)
+            attend(ahead if k < 2 else back, p)
+
+            @pl.when(d == half - 2)
+            def _(k=k):
+                back_dact(k * portion)
 
         pl.when(d == 1)(w_first)
         pl.when(d == 2)(w_second)
         pl.when(d == 4)(w_third)
-        pl.when(d == 5)(w_fourth)
-        pl.when(d == half - 2)(w_done)
-
-        @pl.when(d > half - 3)
-        def _():
-            back_dact((d - half + 2) * portion)
-
+        pl.when(d == 5)(w_done)
         return carry
 
     lax.fori_loop(1, half, step, 0)
-
-    def rest(i, carry):
-        slot = jnp.where(i < 2, z + nz - (half - 1), z + half - 1) % nz
-        attend(slot, i % 2)
-        return carry
-
-    lax.fori_loop(0, 4, rest, 0)
-    local(17).wait()
-    local(18).wait()
+    for p in range(2):
+        attend((z + half - 1) % nz, p)
+    local(11).wait()
+    local(12).wait()
     for p in range(2):
         kv_landed(0, p, half, 0).wait_recv()
         kv_landed(1, p, half, 1).wait_recv()
@@ -491,8 +498,6 @@
         scratch_shapes=[
             pltpu.VMEM((2, nz, 2, 2, BLK, BLK), BF16),
             pltpu.VMEM((2, 2, BLK, BLK), BF16),
-            pltpu.VMEM((2, 2, BLK, BLK), BF16),
-            pltpu.VMEM((2, BLK, BLK), BF16),
             pltpu.VMEM((2,) + w1.shape, BF16),
             pltpu.SMEM(cols.shape, cols.dtype),
             pltpu.VMEM(mask.shape, mask.dtype),
@@ -506,7 +511,7 @@
             pltpu.VMEM((2, BLK, BLK), BF16),
             pltpu.VMEM((2, BLK, BLK), BF16),
             pltpu.VMEM((2, BLK, BLK), BF16),
-            dma((21 + db,)),
+            dma((15 + db,)),
             dma((2, 2, half, 2)),
             dma((2, 2, half, 2)),
             dma((6,)),
@@ -532,14 +537,18 @@
 
 
 def mlp_kernel(
-    rows_ref,
-    cols_ref,
+    rows_any,
+    cols_any,
     hidden_ref,
     dact_ref,
     gblk,
     gain_ref,
     w1,
     w2,
+    out_hbm,
+    gin_hbm,
+    rows_ref,
+    cols_ref,
     out_ref,
     gin_ref,
     normed,
@@ -548,7 +557,14 @@
     dn_acc,
     act,
     dpre,
+    sems,
 ):
+    tables = [
+        pltpu.make_async_copy(rows_any, rows_ref, sems.at[0]),
+        pltpu.make_async_copy(cols_any, cols_ref, sems.at[1]),
+    ]
+    for copy in tables:
+        copy.start()
     hidden = hidden_ref[...]
     mean = jnp.mean(hidden, axis=1, keepdims=True)
     removed = hidden - mean
@@ -562,59 +578,59 @@
         normed[b] = normed_rows[:, cut]
         mlp_acc[b] = hidden[:, cut]
         dn_acc[b] = jnp.zeros((BLK, BLK), F32)
-
-    fb = w1.shape[0]
-    group = 4
-
-    def first(i, carry):
-        for u in range(group):
-            c = i * group + u
-            picked = jnp.concatenate(
-                [normed[rows_ref[0, c]], normed[rows_ref[1, c]]], axis=1
-            )
-            pre = jnp.dot(
-                picked, w1[c].reshape(2 * BLK, BLK), preferred_element_type=F32
-            )
-            phi = 0.5 * (1.0 + lax.erf(pre * 0.7071067811865476))
-            act[c] = (pre * phi).astype(BF16)
-            slope = phi + pre * jnp.exp(-0.5 * pre * pre) * 0.3989422804014327
-            dpre[c] = (dact_ref[c] * slope).astype(BF16)
-        return carry
-
-    lax.fori_loop(0, fb // group, first, 0)
-
-    def second(i, carry):
-        for u in range(group):
-            c = i * group + u
-            w2c = jnp.concatenate([w2[c, 0], w2[c, 1]], axis=1)
-            fpart = jnp.dot(act[c], w2c, preferred_element_type=F32)
-            mlp_acc[cols_ref[0, c]] += fpart[:, :BLK]
-            mlp_acc[cols_ref[1, c]] += fpart[:, BLK:]
-            bpart = lax.dot_general(
-                dpre[c], w1[c].reshape(2 * BLK, BLK), NT, preferred_element_type=F32
-            )
-            dn_acc[rows_ref[0, c]] += bpart[:, :BLK]
-            dn_acc[rows_ref[1, c]] += bpart[:, BLK:]
-        return carry
-
-    lax.fori_loop(0, fb // group, second, 0)
+    for copy in tables:
+        copy.wait()
+
+    for c in range(w1.shape[0]):
+        picked = jnp.concatenate(
+            [normed[rows_ref[0, c]], normed[rows_ref[1, c]]], axis=1
+        )
+        pre = jnp.dot(picked, w1[c].reshape(2 * BLK, BLK), preferred_element_type=F32)
+        phi = 0.5 * (1.0 + lax.erf(pre * 0.7071067811865476))
+        act[c] = (pre * phi).astype(BF16)
+        slope = phi + pre * jnp.exp(-0.5 * pre * pre) * 0.3989422804014327
+        dpre[c] = (dact_ref[c] * slope).astype(BF16)
+
+    for c in range(w1.shape[0]):
+        w2c = jnp.concatenate([w2[c, 0], w2[c, 1]], axis=1)
+        fpart = jnp.dot(act[c], w2c, preferred_element_type=F32)
+        mlp_acc[cols_ref[0, c]] += fpart[:, :BLK]
+        mlp_acc[cols_ref[1, c]] += fpart[:, BLK:]
+        bpart = lax.dot_general(
+            dpre[c], w1[c].reshape(2 * BLK, BLK), NT, preferred_element_type=F32
+        )
+        dn_acc[rows_ref[0, c]] += bpart[:, :BLK]
+        dn_acc[rows_ref[1, c]] += bpart[:, BLK:]
 
     for b in range(db):
         out_ref[:, b * BLK : (b + 1) * BLK] = mlp_acc[b].astype(BF16)
-    dx = jnp.concatenate([dn_acc[b] for b in range(db)], axis=1) * gain_ref[...]
-    unit = xhat[...]
-    inner = (
-        dx
-        - jnp.mean(dx, axis=1, keepdims=True)
-        - unit * jnp.mean(dx * unit, axis=1, keepdims=True)
-    )
-    grad = jnp.concatenate([gblk[b] for b in range(db)], axis=1)
-    gin_ref[...] = (grad.astype(F32) + rstd * inner).astype(BF16)
+    stores = [pltpu.make_async_copy(out_ref, out_hbm, sems.at[2])]
+    stores[0].start()
+    parts = 2
+    size = BLK // parts
+    for i in range(parts):
+        some = slice(i * size, (i + 1) * size)
+        dx = jnp.concatenate([dn_acc[b, some] for b in range(db)], axis=1)
+        dx = dx * gain_ref[...]
+        unit = xhat[some]
+        inner = (
+            dx
+            - jnp.mean(dx, axis=1, keepdims=True)
+            - unit * jnp.mean(dx * unit, axis=1, keepdims=True)
+        )
+        grad = jnp.concatenate([gblk[b, some] for b in range(db)], axis=1)
+        gin_ref[some] = (grad.astype(F32) + rstd[some] * inner).astype(BF16)
+        stores.append(
+            pltpu.make_async_copy(gin_ref.at[some], gin_hbm.at[some], sems.at[3 + i])
+        )
+        stores[-1].start()
+    for copy in stores:
+        copy.wait()
 
 
 def mlp_layer(rows, cols, hidden, dact, gblk, gain, w1, w2):
     vmem_spec = pl.BlockSpec(memory_space=pltpu.VMEM)
-    smem_spec = pl.BlockSpec(memory_space=pltpu.SMEM)
+    any_spec = pl.BlockSpec(memory_space=pl.ANY)
     db = D // BLK
     fb = w1.shape[0]
     out = jax.ShapeDtypeStruct(hidden.shape, BF16)
@@ -622,15 +638,20 @@
         mlp_kernel,
         name="mlp_layer",
         out_shape=(out, out),
-        in_specs=[smem_spec, smem_spec] + [vmem_spec] * 6,
-        out_specs=(vmem_spec, vmem_spec),
+        in_specs=[any_spec, any_spec] + [vmem_spec] * 6,
+        out_specs=(any_spec, any_spec),
         scratch_shapes=[
+            pltpu.SMEM(rows.shape, rows.dtype),
+            pltpu.SMEM(cols.shape, cols.dtype),
+            pltpu.VMEM(hidden.shape, BF16),
+            pltpu.VMEM(hidden.shape, BF16),
             pltpu.VMEM((db, BLK, BLK), BF16),
             pltpu.VMEM(hidden.shape, F32),
             pltpu.VMEM((db, BLK, BLK), F32),
             pltpu.VMEM((db, BLK, BLK), F32),
             pltpu.VMEM((fb, BLK, BLK), BF16),
             pltpu.VMEM((fb, BLK, BLK), BF16),
+            pltpu.SemaphoreType.DMA((5,)),
         ],
         compiler_params=pltpu.CompilerParams(vmem_limit_bytes=32 << 20),
     )(rows, cols, hidden, dact, gblk, gain, w1, w2)

time: 75.8 us -> 68 us (0.90)
  Pallas kernels: 75 us -> 67.1 us
    pallas_call x1, Pallas kernels: 68.4 us -> 62.9 us  [gather_attend(): pl.pallas_call(functools.partial(gather_attend_kernel, nz, ny), name='gat...]
    pallas_call x1, Pallas kernels: 6.56 us -> 4.25 us  [mlp_layer(): pl.pallas_call(mlp_kernel, name='mlp_layer', out_shape=(out, out), in_spe...]
where the time goes in v3:
time: 68 us; the launch traced here: 67.8 us
  Pallas kernels  67.1 us (99%)
    pallas_call x1, Pallas kernels, gather_attend(): pl.pallas_call(functools.partial(gather_attend_kernel, nz, ny), name='gat...  62.9 us
    pallas_call x1, Pallas kernels, mlp_layer(): pl.pallas_call(mlp_kernel, name='mlp_layer', out_shape=(out, out), in_spe...  4.25 us

profile of v3, /device:TPU:2, one launch (start us, length us, event | category | flops | bytes accessed | tf_op | source)
XLA Modules:
  0.0 67.8 jit_solution(8473812768196598199)
XLA Ops:
  0.6 0.0 copy-start
  0.6 0.0 copy-start.1
  0.7 62.9 %gather_attend.1 = (f32[128,1024]{1,0:T(8,128)S(1)}, f32[32,128,128]{2,1,0:T(8,128)S(1)}, bf16[8,128,128]{2,1,0:T(8,128)(2,1)S(1)}, f32[1,1024]{1,0:T(1,128)S(1)...) custom-call(s32[2,32]{1,0:T(2,128)} %bitcast.11, bf16[128,512]{1,0:T(8,128)(2,1)} %bitcast.16, ...), custom_call_target="tpu_custom_call" | custom-call | tf_op jit(solution)/shard_map/gather_attend/pallas_call | solution.py:485
  63.6 0.0 copy-done
  63.6 0.0 copy-done.1
  63.6 4.2 %mlp_layer.1 = (bf16[128,1024]{1,0:T(8,128)(2,1)}, bf16[128,1024]{1,0:T(8,128)(2,1)}) custom-call(s32[2,32]{1,0:T(2,128)S(1)} %bitcast.13, s32[2,32]{1,0:T(2,128)S(1)} %bitcast.12, f32[128,1024]{1,0:T(8,128)S(1)} %get-tuple-element.10.hidden_ref, f32[32,128,128]{2,1,0:T(8,128)S(1)} %get-tuple-element.11.dact_ref, ...), custom_call_target="tpu_custom_call" | custom-call | tf_op jit(solution)/shard_map/mlp_layer/pallas_call | solution.py:637
Async XLA Ops:
  0.6 62.9 %copy-start = (s32[32,2]{0,1:T(2,128)S(1)}, s32[32,2]{0,1:T(2,128)}, u32[]{:S(2)}) copy-start(s32[32,2]{0,1:T(2,128)} %param.22) | copy-start | bytes 772
  0.6 62.9 %copy-start.1 = (s32[32,2]{0,1:T(2,128)S(1)}, s32[32,2]{0,1:T(2,128)}, u32[]{:S(2)}) copy-start(s32[32,2]{0,1:T(2,128)} %param.20) | copy-start | bytes 772

commit v4 on v3

--- a/solution.py
+++ b/solution.py
@@ -393,15 +393,12 @@
     portion = fb // 4
 
     def back_dact(first):
-        def one(u, carry):
+        for u in range(portion):
             c = first + u
             c0, c1 = cols_ref[0, c], cols_ref[1, c]
             gsel = jnp.concatenate([gblk[c0], gblk[c1]], axis=1)
             w2c = jnp.concatenate([w2_all[c, 0], w2_all[c, 1]], axis=1)
             dact_ref[c] = lax.dot_general(gsel, w2c, NT, preferred_element_type=F32)
-            return carry
-
-        lax.fori_loop(0, portion, one, 0)
 
     def step(d, carry):
         back = (z + nz - d) % nz
@@ -581,7 +578,10 @@
     for copy in tables:
         copy.wait()
 
-    for c in range(w1.shape[0]):
+    fb = w1.shape[0]
+    skew = 4
+
+    def first(c):
         picked = jnp.concatenate(
             [normed[rows_ref[0, c]], normed[rows_ref[1, c]]], axis=1
         )
@@ -591,16 +591,22 @@
         slope = phi + pre * jnp.exp(-0.5 * pre * pre) * 0.3989422804014327
         dpre[c] = (dact_ref[c] * slope).astype(BF16)
 
-    for c in range(w1.shape[0]):
+    def second(c):
         w2c = jnp.concatenate([w2[c, 0], w2[c, 1]], axis=1)
         fpart = jnp.dot(act[c], w2c, preferred_element_type=F32)
-        mlp_acc[cols_ref[0, c]] += fpart[:, :BLK]
-        mlp_acc[cols_ref[1, c]] += fpart[:, BLK:]
         bpart = lax.dot_general(
             dpre[c], w1[c].reshape(2 * BLK, BLK), NT, preferred_element_type=F32
         )
-        dn_acc[rows_ref[0, c]] += bpart[:, :BLK]
-        dn_acc[rows_ref[1, c]] += bpart[:, BLK:]
+        for n in range(2):
+            cut = slice(n * BLK, (n + 1) * BLK)
+            mlp_acc[cols_ref[n, c]] += fpart[:, cut]
+            dn_acc[rows_ref[n, c]] += bpart[:, cut]
+
+    for c in range(fb + skew):
+        if c < fb:
+            first(c)
+        if c >= skew:
+            second(c - skew)
 
     for b in range(db):
         out_ref[:, b * BLK : (b + 1) * BLK] = mlp_acc[b].astype(BF16)

time: 68 us -> 67.5 us (level)
  no operation moved by 1% of the time
where the time goes in v4:
time: 67.5 us; the launch traced here: 67.3 us
  Pallas kernels  66.7 us (99%)
    pallas_call x1, Pallas kernels, gather_attend(): pl.pallas_call(functools.partial(gather_attend_kernel, nz, ny), name='gat...  62.9 us
    pallas_call x1, Pallas kernels, mlp_layer(): pl.pallas_call(mlp_kernel, name='mlp_layer', out_shape=(out, out), in_spe...  3.76 us

profile of v4, /device:TPU:2, one launch (start us, length us, event | category | flops | bytes accessed | tf_op | source)
XLA Modules:
  0.0 67.3 jit_solution(6959789310149152415)
XLA Ops:
  0.6 0.0 copy-start
  0.6 0.0 copy-start.1
  0.7 62.9 %gather_attend.1 = (f32[128,1024]{1,0:T(8,128)S(1)}, f32[32,128,128]{2,1,0:T(8,128)S(1)}, bf16[8,128,128]{2,1,0:T(8,128)(2,1)S(1)}, f32[1,1024]{1,0:T(1,128)S(1)...) custom-call(s32[2,32]{1,0:T(2,128)} %bitcast.11, bf16[128,512]{1,0:T(8,128)(2,1)} %bitcast.16, ...), custom_call_target="tpu_custom_call" | custom-call | tf_op jit(solution)/shard_map/gather_attend/pallas_call | solution.py:482
  63.6 0.0 copy-done
  63.6 0.0 copy-done.1
  63.6 3.8 %mlp_layer.1 = (bf16[128,1024]{1,0:T(8,128)(2,1)}, bf16[128,1024]{1,0:T(8,128)(2,1)}) custom-call(s32[2,32]{1,0:T(2,128)S(1)} %bitcast.13, s32[2,32]{1,0:T(2,128)S(1)} %bitcast.12, f32[128,1024]{1,0:T(8,128)S(1)} %get-tuple-element.10.hidden_ref, f32[32,128,128]{2,1,0:T(8,128)S(1)} %get-tuple-element.11.dact_ref, ...), custom_call_target="tpu_custom_call" | custom-call | tf_op jit(solution)/shard_map/mlp_layer/pallas_call | solution.py:643
Async XLA Ops:
  0.6 62.9 %copy-start = (s32[32,2]{0,1:T(2,128)S(1)}, s32[32,2]{0,1:T(2,128)}, u32[]{:S(2)}) copy-start(s32[32,2]{0,1:T(2,128)} %param.22) | copy-start | bytes 772
  0.6 62.9 %copy-start.1 = (s32[32,2]{0,1:T(2,128)S(1)}, s32[32,2]{0,1:T(2,128)}, u32[]{:S(2)}) copy-start(s32[32,2]{0,1:T(2,128)} %param.20) | copy-start | bytes 772
